TPU v7x, 128 devices: a whole 4x4x4 slice. The times are simulated.
128 devices in a mesh: row: 4 (over y), col: 32 (over z, x, core).
Axes of the slice: x: 4, y: 4, z: 4, core: 2. Of those that a mesh axis runs over, the one named last changes fastest.
Arguments:
- hidden_in: bfloat16 [32768, 14336], P(('row', 'col')), may hold values from -6 to 6
- out_grad: bfloat16 [32768, 4096], P(('row', 'col')), may hold values from -6 to 6
- proj_in: bfloat16 [14336, 128], replicated, may hold values from -0.046875 to 0.046875
- proj_out: bfloat16 [4096, 128], replicated, may hold values from -0.09375 to 0.09375
- inverse_fisher: float32 [16384, 16384], P('row', 'col'), may hold values from -0.09375 to 0.09375
- queries: float32 [16384, 256], P('col'), may hold values from -6 to 6
- lengths: int32 [256], replicated, may hold values from 32 to 16640, as said below
- offsets: int32 [256], replicated, may hold values from 0 to 32767, as said below
Outputs:
- scores: float32 [256, 256], P(('row', 'col'))
Inputs may be any that keep to these rules, and one draw needn't show every extreme that they name: `lengths`: every sample has 32 tokens or more, and one sample has exactly 32; one sample has exactly half of all slots plus 256, and that is the most. Samples follow one another in slot order, each after 0 to 3 unused slots; slots after the last sample are unused; offsets[s] + lengths[s] <= 32768.
All inputs are finite; a program needn't handle non-finite values.
Results may differ from a plain program's by a relative error of at most 0.0003.
Values sent between devices are 32-bit elements; how exact they have to be, the bound alone decides.
A program may use at most 128 MiB of HBM per device.

v0:
```python
import jax
import jax.numpy as jnp
from jax import lax
from jax.sharding import Mesh
from jax.sharding import PartitionSpec as P

WINDOW = 9
COL = ("col_0", "col_1", "col_2")
ROW_COL = ("row", "col_0", "col_1", "col_2")


score_scale = 0.0625


def padded_to(lines, count):
    spare = -len(lines) % count
    return jnp.pad(lines, [(0, spare)] + [(0, 0)] * (lines.ndim - 1))


def copy_for_each(shard, axis):
    count = lax.axis_size(axis)
    return lax.all_to_all(
        jnp.broadcast_to(shard[None], (count, *shard.shape)), axis, 0, 0, tiled=True
    )


def in_order(parts, dim):
    parts = jnp.moveaxis(parts, 0, dim)
    shape = parts.shape
    return parts.reshape(*shape[:dim], shape[dim] * shape[dim + 1], *shape[dim + 2 :])


def gathered_by_axis(shard, axes, dim):
    far, near = axes
    parts = copy_for_each(copy_for_each(shard, far), near)
    return in_order(parts.swapaxes(0, 1).reshape(-1, *shard.shape), dim)


def cut_along(shard, dim, count):
    shape = shard.shape
    parts = shard.reshape(*shape[:dim], count, shape[dim] // count, *shape[dim + 1 :])
    return jnp.moveaxis(parts, dim, 0)


def summed_on_arrival(shard, axis, dim):
    count = lax.axis_size(axis)
    parts = lax.all_to_all(cut_along(shard, dim, count), axis, 0, 0, tiled=True)
    return jnp.sum(parts, axis=0)


def sum_in_two_steps(shard, axes, dim):
    far, near = axes
    parts = cut_along(shard, dim, lax.axis_size(far))
    nearer = summed_on_arrival(parts, near, dim + 1)
    arrived = lax.all_to_all(nearer, far, split_axis=0, concat_axis=0, tiled=True)
    return arrived.sum(axis=0)


def nested_sum(shard, axes):
    lines = shard.reshape(-1, shard.shape[-1])
    padded = padded_to(lines, lax.axis_size(axes[0]) * lax.axis_size(axes[1]))
    whole = gathered_by_axis(sum_in_two_steps(padded, axes, 0), axes, 0)
    return lax.slice_in_dim(whole, 0, len(lines)).reshape(shard.shape)


def exact_dot(left, right):
    return jnp.dot(left, right, precision=lax.Precision.HIGHEST, preferred_element_type=jnp.float32)


def body(hidden_in, out_grad, proj_in, proj_out, inverse_fisher, queries, lengths, offsets):
    tok_rows = hidden_in.shape[0]
    proj_tokens = jnp.dot(hidden_in, proj_in, preferred_element_type=jnp.float32)
    proj_grads = jnp.dot(out_grad, proj_out, preferred_element_type=jnp.float32)
    row_count = lax.axis_size("row")
    col_count = lax.axis_size(COL)
    row_id = lax.axis_index("row")
    col_id = lax.axis_index(COL)
    samples = lengths.shape[0]
    sample_ends = offsets + lengths

    def window_start(device):
        first_slot = device * tok_rows
        passed = jnp.sum((sample_ends <= first_slot).astype(jnp.int32))
        return jnp.minimum(passed, samples - WINDOW)

    device_id = row_id * col_count + col_id
    first_sample = window_start(device_id)
    win_offsets = lax.dynamic_slice_in_dim(offsets, first_sample, WINDOW, 0)
    win_ends = lax.dynamic_slice_in_dim(sample_ends, first_sample, WINDOW, 0)
    positions = device_id * tok_rows + jnp.arange(tok_rows, dtype=jnp.int32)
    member = (
        (positions[None, :] >= win_offsets[:, None]) & (positions[None, :] < win_ends[:, None])
    ).astype(jnp.float32)
    weighted = member[:, :, None] * proj_grads[None, :, :]
    window_grads = jnp.einsum(
        "wta,tb->wab", weighted, proj_tokens, precision=lax.Precision.HIGHEST
    ).reshape(WINDOW, -1)
    sample_axis = jnp.arange(samples, dtype=jnp.int32)
    u_block = nested_sum(exact_dot(inverse_fisher, queries), (("col_0", "col_1"), "col_2"))
    received = lax.all_to_all(window_grads, "row", split_axis=1, concat_axis=0, tiled=True)
    partial_value = exact_dot(received, u_block)
    peer_ids = jnp.arange(row_count, dtype=jnp.int32) * col_count + col_id
    peer_first = jax.vmap(window_start)(peer_ids)
    targets = (peer_first[:, None] + jnp.arange(WINDOW, dtype=jnp.int32)[None, :]).reshape(-1)
    onehot = (sample_axis[:, None] == targets[None, :]).astype(jnp.float32)
    score_terms = exact_dot(onehot, partial_value)
    owned_scores = sum_in_two_steps(score_terms, (("row", "col_0", "col_1"), "col_2"), 0)
    owned_rows = owned_scores.shape[0]
    owned_lengths = lax.dynamic_slice_in_dim(lengths, device_id * owned_rows, owned_rows, 0)
    return score_scale * owned_scores / owned_lengths.astype(jnp.float32)[:, None]


def solution(mesh):
    split = Mesh(
        mesh.devices.reshape(mesh.shape["row"], 4, 4, 2), ("row", "col_0", "col_1", "col_2")
    )
    return jax.shard_map(
        body,
        mesh=split,
        in_specs=(
            P(ROW_COL, None),
            P(ROW_COL, None),
            P(),
            P(),
            P("row", COL),
            P(COL, None),
            P(),
            P(),
        ),
        out_specs=P(ROW_COL, None),
        check_vma=False,
    )
```

profile of v0, /device:TPU:1, one launch (start us, length us, event | category | flops | bytes accessed | tf_op | source)
XLA Modules:
  0.0 149.5 jit_solution(5360597075745093286)
XLA Ops:
  0.0 9.4 %fusion.8 = f32[4096,256]{1,0:T(8,128)S(1)} fusion(f32[4096,512]{1,0:T(8,128)} %param.12, f32[512,256]{1,0:T(8,128)} %param.13), kind=kOutput, calls=%fused_computation.21 | convolution fusion | flops 6442450944 | bytes 13107200 | tf_op jit(solution)/shard_map/dot_general | solution.py:67
  9.4 0.4 copy.30
  9.9 9.2 %all_to_all.49 = f32[2,16,128,256]{3,2,1,0:T(8,128)} all-to-all(f32[2,16,128,256]{3,2,1,0:T(8,128)S(1)} %bitcast.25), channel_id=1, replica_groups=mesh['row'=4,'col_0'=4,'col_1'=4,'col_2'=2] {'col_2'}, dimensions={0} | all-to-all | bytes 8388608 | tf_op jit(solution)/shard_map/all_to_all | solution.py:47
  19.1 4.1 %reduce_sum.56 = f32[16,128,256]{2,1,0:T(8,128)} reduce(f32[2,16,128,256]{3,2,1,0:T(8,128)} %all_to_all.49, f32[]{:T(128)} %constant.32.clone.1), dimensions={0}, to_apply=%region_2.3 | reduce | flops 524288 | bytes 6291460 | tf_op jit(solution)/shard_map/reduce_sum | solution.py:48
  23.2 7.8 %all-to-all-start.2 = ((f32[16,128,256]{2,1,0:T(8,128)}), f32[16,128,256]{2,1,0:T(8,128)}, u32[]{:S(2)}, u32[]{:S(2)}) async-start(f32[16,128,256]{2,1,0:T(8,128)} %reduce_sum.56), calls=%async_computation.2 | async-start | bytes 4194304 | tf_op jit(solution)/shard_map/all_to_all | solution.py:55
  31.0 0.6 fusion.6
  32.5 0.8 fusion.7
  33.3 6.3 %convolution_bitcast_fusion = f32[256,128,1]{1,0,2:T(8,128)S(1)} fusion(bf16[256,14336]{1,0:T(8,128)(2,1)} %param.8, bf16[14336,128]{1,0:T(8,128)(2,1)} %param.10), kind=kOutput, calls=%fused_computation.3 | convolution fusion | flops 939524096 | bytes 11141120 | tf_op jit(solution)/shard_map/dot_general | solution.py:72
  39.7 1.1 fusion
  40.8 0.2 all_to_all.32
  41.0 1.3 copy.21
  42.3 20.8 %all-to-all-done.2 = f32[16,128,256]{2,1,0:T(8,128)} async-done(((f32[16,128,256]{2,1,0:T(8,128)}), f32[16,128,256]{2,1,0:T(8,128)}, u32[]{:S(2)}, u32[]{:S(2)}) %all-to-all-start.2) | async-done | bytes 2097184 | tf_op jit(solution)/shard_map/all_to_all | solution.py:55
  63.1 4.2 %all-to-all-start = ((f32[9,4,4096]{2,0,1:T(8,128)}), f32[9,4,4096]{2,0,1:T(8,128)S(1)}, u32[]{:S(2)}, u32[]{:S(2)}) async-start(f32[9,4,4096]{2,0,1:T(8,128)} %copy.21), calls=%async_computation | async-start | bytes 2097152 | tf_op jit(solution)/shard_map/all_to_all | solution.py:100
  67.3 1.7 %reduce_sum.57 = f32[128,256]{1,0:T(8,128)S(1)} reduce(f32[16,128,256]{2,1,0:T(8,128)} %all-to-all-done.2, f32[]{:T(128)} %constant.32.clone.1), dimensions={0}, to_apply=%region_3.4 | reduce | flops 491520 | bytes 2228228 | tf_op jit(solution)/shard_map/reduce_sum | solution.py:56
  69.0 11.7 %all-to-all-done = f32[9,4,4096]{2,0,1:T(8,128)S(1)} async-done(((f32[9,4,4096]{2,0,1:T(8,128)}), f32[9,4,4096]{2,0,1:T(8,128)S(1)}, u32[]{:S(2)}, u32[]{:S(2)}) %all-to-all-start) | async-done | bytes 589856 | tf_op jit(solution)/shard_map/all_to_all | solution.py:100
  80.7 1.5 %broadcast_in_dim.4 = f32[16,128,256]{2,1,0:T(8,128)} broadcast(f32[128,256]{1,0:T(8,128)S(1)} %reduce_sum.57), dimensions={1,2} | broadcast | bytes 2228224 | tf_op jit(solution)/shard_map/broadcast_in_dim | solution.py:23
  82.2 4.4 %all-to-all-start.3 = ((f32[16,128,256]{2,1,0:T(8,128)}), f32[16,128,256]{2,1,0:T(8,128)}, u32[]{:S(2)}, u32[]{:S(2)}) async-start(f32[16,128,256]{2,1,0:T(8,128)} %broadcast_in_dim.4), calls=%async_computation.3 | async-start | bytes 4194304 | tf_op jit(solution)/shard_map/all_to_all | solution.py:22
  86.7 0.2 convert_reduce_fusion
  87.0 0.9 all_to_all.35
  88.0 24.3 %all-to-all-done.3 = f32[16,128,256]{2,1,0:T(8,128)} async-done(((f32[16,128,256]{2,1,0:T(8,128)}), f32[16,128,256]{2,1,0:T(8,128)}, u32[]{:S(2)}, u32[]{:S(2)}) %all-to-all-start.3) | async-done | bytes 2097184 | tf_op jit(solution)/shard_map/all_to_all | solution.py:22
  112.3 2.1 %broadcast_in_dim.5 = f32[2,16,128,256]{3,2,1,0:T(8,128)S(1)} broadcast(f32[16,128,256]{2,1,0:T(8,128)} %all-to-all-done.3), dimensions={1,2,3} | broadcast | bytes 6291456 | tf_op jit(solution)/shard_map/broadcast_in_dim | solution.py:23
  114.4 12.5 %all_to_all.50 = f32[2,16,128,256]{3,2,1,0:T(8,128)S(1)} all-to-all(f32[2,16,128,256]{3,2,1,0:T(8,128)S(1)} %broadcast_in_dim.5), channel_id=1, replica_groups=mesh['row'=4,'col_0'=4,'col_1'=4,'col_2'=2] {'col_2'}, dimensions={0} | all-to-all | bytes 8388608 | tf_op jit(solution)/shard_map/all_to_all | solution.py:22
  126.9 0.4 copy.23
  127.3 0.6 copy-done.1
  128.0 2.2 %fusion.9 = f32[36,256]{1,0:T(8,128)S(1)} fusion(f32[36,4096]{1,0:T(8,128)S(1)} %copy-done.1, f32[4096,256]{1,0:T(8,128)S(1)} %bitcast.24), kind=kOutput, calls=%fused_computation.22 | convolution fusion | flops 452984832 | bytes 4820992 | tf_op jit(solution)/shard_map/dot_general | solution.py:67
  130.1 0.2 fusion.4
  130.4 0.1 reshape_reshape.11
  130.6 3.9 %all_to_all.51 = f32[2,64,2,256]{3,2,1,0:T(2,128)S(1)} all-to-all(f32[2,64,2,256]{3,2,1,0:T(2,128)S(1)} %bitcast.27), channel_id=1, replica_groups=mesh['row'=4,'col_0'=4,'col_1'=4,'col_2'=2] {'col_2'}, dimensions={0} | all-to-all | bytes 524288 | tf_op jit(solution)/shard_map/all_to_all | solution.py:47
  134.5 0.8 reduce_sum.58
  135.3 4.6 %all-to-all-start.6 = ((f32[64,2,256]{2,1,0:T(2,128)}), f32[64,2,256]{2,1,0:T(2,128)S(1)}, u32[]{:S(2)}, u32[]{:S(2)}) async-start(f32[64,2,256]{2,1,0:T(2,128)} %reduce_sum.58), calls=%async_computation.6 | async-start | bytes 262144 | tf_op jit(solution)/shard_map/all_to_all | solution.py:55
  140.0 8.7 %all-to-all-done.6 = f32[64,2,256]{2,1,0:T(2,128)S(1)} async-done(((f32[64,2,256]{2,1,0:T(2,128)}), f32[64,2,256]{2,1,0:T(2,128)S(1)}, u32[]{:S(2)}, u32[]{:S(2)}) %all-to-all-start.6) | async-done | bytes 131104 | tf_op jit(solution)/shard_map/all_to_all | solution.py:55
  148.8 0.7 multiply_divide_fusion
  (19 shorter events, 0.6 us)
Async XLA Ops:
  0.0 32.5 %copy-start = (bf16[256,4096]{1,0:T(8,128)(2,1)S(1)}, bf16[256,4096]{1,0:T(8,128)(2,1)}, u32[]{:S(2)}) copy-start(bf16[256,4096]{1,0:T(8,128)(2,1)} %param.9) | copy-start | bytes 6291460
  19.0 11.9 %copy-start.3 = (s32[256]{0:T(256)S(1)}, s32[256]{0:T(256)}, u32[]{:S(2)}) copy-start(s32[256]{0:T(256)} %param.15) | copy-start | bytes 3076
  19.0 11.9 %copy-start.4 = (s32[256]{0:T(256)S(1)}, s32[256]{0:T(256)}, u32[]{:S(2)}) copy-start(s32[256]{0:T(256)} %param.14) | copy-start | bytes 3076
  19.1 13.5 %copy-start.2 = (bf16[4096,128]{1,0:T(8,128)(2,1)S(1)}, bf16[4096,128]{1,0:T(8,128)(2,1)}, u32[]{:S(2)}) copy-start(bf16[4096,128]{1,0:T(8,128)(2,1)} %param.11) | copy-start | bytes 3145732
  23.2 39.9 %all-to-all-start.2 = ((f32[16,128,256]{2,1,0:T(8,128)}), f32[16,128,256]{2,1,0:T(8,128)}, u32[]{:S(2)}, u32[]{:S(2)}) async-start(f32[16,128,256]{2,1,0:T(8,128)} %reduce_sum.56), calls=%async_computation.2 | async-start | bytes 4194304 | tf_op jit(solution)/shard_map/all_to_all | solution.py:55
  63.1 17.6 %all-to-all-start = ((f32[9,4,4096]{2,0,1:T(8,128)}), f32[9,4,4096]{2,0,1:T(8,128)S(1)}, u32[]{:S(2)}, u32[]{:S(2)}) async-start(f32[9,4,4096]{2,0,1:T(8,128)} %copy.21), calls=%async_computation | async-start | bytes 2097152 | tf_op jit(solution)/shard_map/all_to_all | solution.py:100
  82.2 30.1 %all-to-all-start.3 = ((f32[16,128,256]{2,1,0:T(8,128)}), f32[16,128,256]{2,1,0:T(8,128)}, u32[]{:S(2)}, u32[]{:S(2)}) async-start(f32[16,128,256]{2,1,0:T(8,128)} %broadcast_in_dim.4), calls=%async_computation.3 | async-start | bytes 4194304 | tf_op jit(solution)/shard_map/all_to_all | solution.py:22
  126.9 1.1 copy-start.1
  135.3 13.4 %all-to-all-start.6 = ((f32[64,2,256]{2,1,0:T(2,128)}), f32[64,2,256]{2,1,0:T(2,128)S(1)}, u32[]{:S(2)}, u32[]{:S(2)}) async-start(f32[64,2,256]{2,1,0:T(2,128)} %reduce_sum.58), calls=%async_computation.6 | async-start | bytes 262144 | tf_op jit(solution)/shard_map/all_to_all | solution.py:55
where the time goes:
time: 150 us; the launch traced here: 149 us
  waiting for transfers between devices  65.5 us (44%)
  blocking collectives  25.6 us (17%)
  starting transfers between devices  21 us (14%)
  matrix products  20 us (13%)
  other arithmetic  8.47 us (6%)
  local copies, waits for them, and re-layouts  8.02 us (5%)
    all_to_all x2, waiting for transfers between devices, sum_in_two_steps(): lax.all_to_all(nearer, far, split_axis=0, concat_axis=0, tiled=True)  29.5 us
    all_to_all x1, waiting for transfers between devices, copy_for_each(): lax.all_to_all(jnp.broadcast_to(shard[None], (count, *shard.shape)), axis...  24.3 us
    all_to_all x2, blocking collectives, summed_on_arrival(): parts = lax.all_to_all(cut_along(shard, dim, count), axis, 0, 0, tiled=True)  13.1 us
    all_to_all x1, blocking collectives, copy_for_each(): lax.all_to_all(jnp.broadcast_to(shard[None], (count, *shard.shape)), axis...  12.5 us
    all_to_all x2, starting transfers between devices, sum_in_two_steps(): lax.all_to_all(nearer, far, split_axis=0, concat_axis=0, tiled=True)  12.4 us
    dot_general x3, matrix products, exact_dot(): jnp.dot(left, right, precision=lax.Precision.HIGHEST, preferred_element_t...  11.8 us
    all_to_all x1, waiting for transfers between devices, body(): lax.all_to_all(window_grads, 'row', split_axis=1, concat_axis=0, tiled=True)  11.7 us
    dot_general x1, matrix products, body(): jnp.dot(hidden_in, proj_in, preferred_element_type=jnp.float32)  6.33 us
  transfers between devices with their start and end apart: 4, of which 4 were waited for; matrix products, arithmetic and copies ran while one was open for 8% of the time, Pallas kernels for 0%

commit v1 on v0

v1 whole, which is shorter than its diff:
```python
import functools

import jax
import jax.numpy as jnp
from jax import lax
from jax.experimental import pallas as pl
from jax.experimental.pallas import tpu as pltpu
from jax.sharding import Mesh
from jax.sharding import PartitionSpec as P

AXES = ("row", "col_0", "col_1", "col_2")
WIN = 17
PITCH = 24
KCH = 2048
score_scale = 0.0625
f32 = jnp.float32
bf16 = jnp.bfloat16


def split(v):
    hi = v.astype(bf16)
    lo = (v - hi.astype(f32)).astype(bf16)
    return hi, lo


def dot(a, b):
    return jnp.dot(a, b, preferred_element_type=f32)


def kernel(
    f_ref, q_ref, h_ref, pi_ref, g_ref, po_ref, off_ref, len_ref, lens_ref,
    out_ref,
    fv, qv, hv, piv, gv, pov, q3,
    ua, ub, ca, cb,
    fa1, fb1, na1, nb1, fa2, fb2, na2, nb2,
    pt, pg, pgt, gsend, grecv, oneh, sbuf, srecv, sown, spart,
    fsem, qsem, hsem, gsem,
    csend, crecv, r_send, r_recv,
    psend, precv, gssem, grsem, sssem, srsem, xsend, xrecv,
):
    y = lax.axis_index("row")
    z = lax.axis_index("col_0")
    x = lax.axis_index("col_1")
    k = lax.axis_index("col_2")
    chip = y * 16 + z * 4 + x

    def remote(src, dst, ss, rs, dev):
        return pltpu.make_async_remote_copy(
            src_ref=src, dst_ref=dst, send_sem=ss, recv_sem=rs,
            device_id=dev, device_id_type=pl.DeviceIdType.MESH,
        )

    partner = (y, z, x, lax.rem(k + 1, 2))
    xp = (y, z, lax.rem(x + 1, 4), k)
    xm = (y, z, lax.rem(x + 3, 4), k)
    zp = (y, lax.rem(z + 1, 4), x, k)
    zm = (y, lax.rem(z + 3, 4), x, k)

    grecv[...] = jnp.zeros_like(grecv)

    barrier = pltpu.get_barrier_semaphore()

    @pl.loop(1, 128)
    def _(o):
        pl.semaphore_signal(
            barrier, inc=1,
            device_id=(
                lax.rem(y + o // 32, 4),
                lax.rem(z + (o // 8) % 4, 4),
                lax.rem(x + (o // 2) % 4, 4),
                lax.rem(k + o % 2, 2),
            ),
            device_id_type=pl.DeviceIdType.MESH,
        )

    qcopy = pltpu.make_async_copy(q_ref, qv, qsem.at[0])
    qcopy.start()

    def fcopy(g, dz):
        dk = 1 - g // 4
        dx = (6 - g % 4) % 4
        a = lax.rem(k + dk, 2) * 16 + lax.rem(x + dx, 4) * 4 + lax.rem(z + dz, 4)
        rows = pl.ds(pl.multiple_of(a * 128, 128), 128)
        return pltpu.make_async_copy(f_ref.at[rows], fv.at[g, dz], fsem.at[g, dz])

    @pl.loop(0, 32)
    def _(i):
        fcopy(i // 4, i % 4).start()

    def hcopies(c):
        cols = pl.ds(pl.multiple_of(c * KCH, KCH), KCH)
        return (
            pltpu.make_async_copy(h_ref.at[:, cols], hv.at[c], hsem.at[0, c]),
            pltpu.make_async_copy(pi_ref.at[cols], piv.at[c], hsem.at[1, c]),
        )

    def gcopies(c):
        cols = pl.ds(pl.multiple_of(c * KCH, KCH), KCH)
        return (
            pltpu.make_async_copy(g_ref.at[:, cols], gv.at[c], gsem.at[0, c]),
            pltpu.make_async_copy(po_ref.at[cols], pov.at[c], gsem.at[1, c]),
        )

    @pl.loop(0, 2)
    def _(c):
        for cp in gcopies(c):
            cp.start()

    @pl.loop(0, 7)
    def _(c):
        for cp in hcopies(c):
            cp.start()

    qcopy.wait()
    qh, ql = split(qv[...])
    q3[0:512] = qh
    q3[512:1024] = ql
    q3[1024:1536] = qh

    @pl.loop(0, 8)
    def _(g):
        for dz in range(4):
            fcopy(g, dz).wait()
        dk = 1 - g // 4
        dx = (6 - g % 4) % 4
        hi, lo = split(fv[g].reshape(512, 512))
        u = dot(jnp.concatenate([hi, hi, lo], axis=1), q3[...]).reshape(4, 128, 256)
        ua[dk, dx] = u[:, 0:64]
        for dz in range(4):
            ub[dk, dz, dx] = u[dz, 64:128]

    pl.semaphore_wait(barrier, 127)

    order = (2, 1, 3, 0)
    swaps = {}
    for n, q in enumerate(order):
        for c, (u, r) in enumerate(((ua, ca), (ub, cb))):
            cp = remote(u.at[1, q], r.at[q], csend.at[c, q], crecv.at[c, q], partner)
            cp.start()
            swaps[c, q] = cp

    done = list(swaps.values())

    def merge(c, q):
        u, r = ((ua, ca), (ub, cb))[c]
        swaps[c, q].wait_recv()
        u[0, q] = u[0, q] + r[q]

    class Ring:
        def __init__(self, p, half, far, near, ids, plus, minus):
            self.p, self.half, self.far, self.near = p, half, far, near
            self.ids, self.plus, self.minus = ids, plus, minus
            self.recv = {}

        def piece(self, q, h):
            return self.p.at[q, pl.ds(h * self.half, self.half)]

        def go(self, name, n, src, dst, dev):
            cp = remote(src, dst, r_send.at[self.ids, n], r_recv.at[self.ids, n], dev)
            cp.start()
            self.recv[name] = cp
            done.append(cp)

        def send_far(self):
            self.go("f0", 0, self.piece(2, 0), self.far.at[0], self.plus)
            self.go("f1", 1, self.piece(2, 1), self.far.at[1], self.minus)

        def part(self, i, h):
            return self.near.at[i, pl.ds(h * self.half, self.half)]

        def send_plus_early(self):
            self.go("p1", 2, self.piece(1, 1), self.part(0, 1), self.plus)

        def send_minus_early(self):
            self.go("m0", 3, self.piece(3, 0), self.part(1, 0), self.minus)

        def relay(self):
            self.recv["f0"].wait_recv()
            s = self.piece(1, 0)
            s[...] = s[...] + self.far[0]
            self.go("p0", 4, s, self.part(0, 0), self.plus)
            self.recv["f1"].wait_recv()
            s = self.piece(3, 1)
            s[...] = s[...] + self.far[1]
            self.go("m1", 5, s, self.part(1, 1), self.minus)

        def finish(self):
            for name in ("p1", "m0", "p0", "m1"):
                self.recv[name].wait_recv()
            self.p[0] = self.p[0] + self.near[0] + self.near[1]

    ring_a = Ring(ua.at[0], 2, fa1, na1, 0, xp, xm)
    ring_b = Ring(ub.at[0], 2, fb1, nb1, 1, zp, zm)
    ring_a2 = Ring(ua.at[0, 0], 32, fa2, na2, 2, zp, zm)
    ring_b2 = Ring(ub.at[0, 0], 32, fb2, nb2, 3, xp, xm)

    merge(0, 2)
    ring_a.send_far()
    merge(1, 2)
    ring_b.send_far()
    merge(0, 1)
    ring_a.send_plus_early()
    merge(1, 1)
    ring_b.send_plus_early()
    merge(0, 3)
    ring_a.send_minus_early()
    merge(1, 3)
    ring_b.send_minus_early()
    merge(0, 0)
    merge(1, 0)

    mine = pl.ds(pl.multiple_of(k * 256, 256), 256)
    pg[mine] = jnp.zeros((256, 128), f32)
    pt[mine] = jnp.zeros((256, 128), f32)

    @pl.loop(0, 2)
    def _(c):
        for cp in gcopies(c):
            cp.wait()
        pg[mine] = pg[mine] + dot(gv[c], pov[c])

    @pl.loop(0, 7)
    def _(c):
        for cp in hcopies(c):
            cp.wait()
        pt[mine] = pt[mine] + dot(hv[c], piv[c])

    give_g = remote(pg.at[mine], pg.at[mine], psend.at[0], precv.at[0], partner)
    give_t = remote(pt.at[mine], pt.at[mine], psend.at[1], precv.at[1], partner)
    give_g.start()
    give_t.start()
    done.extend((give_g, give_t))

    ring_a.relay()
    ring_b.relay()

    off_row = off_ref[...].astype(f32)
    end_row = off_row + len_ref[...].astype(f32)
    off_col = jnp.transpose(jnp.broadcast_to(off_row, (8, 256)))[:, 0:1]
    end_col = jnp.transpose(jnp.broadcast_to(end_row, (8, 256)))[:, 0:1]
    slot0 = (chip * 512).astype(f32)
    slots = lax.broadcasted_iota(jnp.int32, (1, 512), 1).astype(f32) + slot0
    begun = jnp.sum((off_col <= slots).astype(f32), axis=0, keepdims=True)
    ended = jnp.sum((end_col <= slots).astype(f32), axis=0, keepdims=True)
    passed = jnp.sum((end_col <= slot0).astype(f32), axis=0, keepdims=True)
    window = jnp.where(begun == ended + 1.0, begun - 1.0 - passed, -1.0)
    member = (
        lax.broadcasted_iota(jnp.int32, (PITCH, 512), 0).astype(f32) == window
    ).astype(f32)

    give_g.wait_recv()
    give_t.wait_recv()
    pgt[...] = jnp.transpose(pg[...]).reshape(8, 16, 512)
    th, tl = split(pt[...])
    t3 = jnp.concatenate([th, tl, th], axis=0)
    for yy in range(4):
        lines = pgt[yy * 2 + k]
        spread = (lines[:, None, :] * member[None, :, :]).reshape(16 * PITCH, 512)
        hi, lo = split(spread)
        grads = dot(jnp.concatenate([hi, hi, lo], axis=1), t3)
        gsend[yy * 16 : yy * 16 + 16] = grads.reshape(16, PITCH, 128)

    def peer(o):
        return (
            lax.rem(y + o // 16, 4),
            lax.rem(z + o % 4, 4),
            lax.rem(x + (o // 4) % 4, 4),
        )

    @pl.loop(1, 64)
    def _(o):
        py, pz, px = peer(o)
        remote(
            gsend.at[py * 16 + px * 4 + pz, pl.ds(0, WIN)],
            grecv.at[chip, pl.ds(0, WIN)],
            gssem.at[0], grsem.at[0], (py, pz, px, k),
        ).start()

    grecv[chip] = gsend[y * 16 + x * 4 + z]

    cols = lax.broadcasted_iota(jnp.int32, (1, 64 * PITCH), 1)
    col_chip = (cols * 2731) >> 16
    col_win = cols - col_chip * PITCH
    col_slot = (col_chip * 512).astype(f32)
    before = jnp.sum((end_col <= col_slot).astype(f32), axis=0, keepdims=True)
    target = jnp.where(col_win < WIN, before + col_win.astype(f32), -1.0)
    line = lax.broadcasted_iota(jnp.int32, (512, 1), 0)
    sample = (line >> 3) * 4 + ((line >> 2) & 1) * 2 + (line & 1)
    oneh[...] = (sample.astype(f32) == target).astype(f32).astype(bf16)

    ring_a.finish()
    ring_a2.send_far()
    ring_a2.send_plus_early()
    ring_a2.send_minus_early()
    ring_b.finish()
    ring_b2.send_far()
    ring_b2.send_plus_early()
    ring_b2.send_minus_early()
    ring_a2.relay()
    ring_b2.relay()
    ring_a2.finish()
    ring_b2.finish()

    uh, ul = split(jnp.concatenate([ua[0, 0, 0], ub[0, 0, 0]], axis=0))
    u3 = jnp.concatenate([uh, ul, uh], axis=0)

    pltpu.make_async_copy(
        grecv.at[pl.ds(0, 63), pl.ds(0, WIN)], grecv.at[pl.ds(0, 63), pl.ds(0, WIN)], grsem.at[0]
    ).wait()
    gh, gl = split(grecv[...].reshape(64 * PITCH, 128))
    dense = dot(oneh[...], gh) + dot(oneh[...], gl)
    dh, dl = split(dense)
    both = dot(jnp.concatenate([dh, dh, dl], axis=1), u3)
    upper = ((line >> 1) & 1) == 0
    sbuf[...] = jnp.where(upper, both[:, 0:128], both[:, 128:256]).reshape(64, 8, 128)

    @pl.loop(1, 64)
    def _(o):
        py, pz, px = peer(o)
        remote(
            sbuf.at[py * 16 + pz * 4 + px], srecv.at[chip],
            sssem.at[0], srsem.at[0], (py, pz, px, k),
        ).start()

    srecv[chip] = sbuf[chip]
    pltpu.make_async_copy(
        srecv.at[pl.ds(0, 63)], srecv.at[pl.ds(0, 63)], srsem.at[0]
    ).wait()
    sown[...] = jnp.sum(srecv[...], axis=0)
    last = remote(sown, spart, xsend.at[0], xrecv.at[0], partner)
    last.start()
    last.wait_recv()
    tile = sown[...] + spart[...]
    tile = jnp.where(k == 0, tile[0:4], tile[4:8]) * score_scale
    d = chip * 2 + k
    for s in range(2):
        n = lens_ref[2 * d + s].astype(f32)
        for j in range(2):
            out_ref[s : s + 1, j * 128 : j * 128 + 128] = tile[j * 2 + s : j * 2 + s + 1] / n

    last.wait_send()
    for cp in done:
        cp.wait_send()
    pltpu.make_async_copy(
        gsend.at[pl.ds(0, 63), pl.ds(0, WIN)], gsend.at[pl.ds(0, 63), pl.ds(0, WIN)], gssem.at[0]
    ).wait()
    pltpu.make_async_copy(sbuf.at[pl.ds(0, 63)], sbuf.at[pl.ds(0, 63)], sssem.at[0]).wait()


def body(hidden_in, out_grad, proj_in, proj_out, inverse_fisher, queries, lengths, offsets):
    vmem = pltpu.VMEM
    dma = pltpu.SemaphoreType.DMA
    anys = pl.BlockSpec(memory_space=pl.ANY)
    invm = pl.BlockSpec(memory_space=pltpu.VMEM)
    return pl.pallas_call(
        kernel,
        out_shape=jax.ShapeDtypeStruct((2, 256), f32),
        in_specs=[anys] * 6 + [invm] * 2 + [pl.BlockSpec(memory_space=pltpu.SMEM)],
        out_specs=invm,
        scratch_shapes=[
            vmem((8, 4, 128, 512), f32), vmem((512, 256), f32),
            vmem((7, 256, KCH), bf16), vmem((7, KCH, 128), bf16),
            vmem((2, 256, KCH), bf16), vmem((2, KCH, 128), bf16),
            vmem((1536, 256), bf16),
            vmem((2, 4, 4, 64, 256), f32), vmem((2, 4, 4, 64, 256), f32),
            vmem((4, 4, 64, 256), f32), vmem((4, 4, 64, 256), f32),
            vmem((2, 2, 64, 256), f32), vmem((2, 2, 64, 256), f32),
            vmem((2, 4, 64, 256), f32), vmem((2, 4, 64, 256), f32),
            vmem((2, 32, 256), f32), vmem((2, 32, 256), f32),
            vmem((2, 64, 256), f32), vmem((2, 64, 256), f32),
            vmem((512, 128), f32), vmem((512, 128), f32), vmem((8, 16, 512), f32),
            vmem((64, PITCH, 128), f32), vmem((64, PITCH, 128), f32),
            vmem((512, 64 * PITCH), bf16),
            vmem((64, 8, 128), f32), vmem((64, 8, 128), f32),
            vmem((8, 128), f32), vmem((8, 128), f32),
            dma((8, 4)), dma((1,)), dma((2, 7)), dma((2, 2)),
            dma((2, 4)), dma((2, 4)), dma((4, 6)), dma((4, 6)),
            dma((2,)), dma((2,)), dma((1,)), dma((1,)), dma((1,)), dma((1,)),
            dma((1,)), dma((1,)),
        ],
        compiler_params=pltpu.CompilerParams(
            collective_id=0, has_side_effects=True, vmem_limit_bytes=60 * 1024 * 1024
        ),
    )(
        inverse_fisher, queries, hidden_in, proj_in, out_grad, proj_out,
        offsets.reshape(1, 256), lengths.reshape(1, 256), lengths,
    )


def solution(mesh):
    whole = Mesh(mesh.devices.reshape(4, 4, 4, 2), AXES)
    col = AXES[1:]
    return jax.shard_map(
        body,
        mesh=whole,
        in_specs=(
            P(AXES, None), P(AXES, None), P(), P(), P("row", col), P(col, None), P(), P(),
        ),
        out_specs=P(AXES, None),
        check_vma=False,
    )
```

time: 150 us -> 54.8 us (0.37)
  waiting for transfers between devices: 65.5 us -> 0 us
  Pallas kernels: 0 us -> 53.4 us
  blocking collectives: 25.6 us -> 0 us
  starting transfers between devices: 21 us -> 0 us
  matrix products: 20 us -> 0 us
  other arithmetic: 8.47 us -> 0 us
  local copies, waits for them, and re-layouts: 8.02 us -> 1.26 us
    all_to_all x4 -> x0, waiting for transfers between devices: 65.5 us -> none  [the longest x2 29.5 us: sum_in_two_steps(): lax.all_to_all(nearer, far, split_axis=0, concat_axis=0, tiled=True)]
    pallas_call x0 -> x1, Pallas kernels: none -> 53.4 us  [body(): pl.pallas_call(kernel, out_shape=jax.ShapeDtypeStruct((2, 256), f32), in_...]
    all_to_all x3 -> x0, blocking collectives: 25.6 us -> none  [the longest x2 13.1 us: summed_on_arrival(): parts = lax.all_to_all(cut_along(shard, dim, count), axis, 0, 0, tiled=True)]
    all_to_all x4 -> x0, starting transfers between devices: 21 us -> none  [the longest x2 12.4 us: sum_in_two_steps(): lax.all_to_all(nearer, far, split_axis=0, concat_axis=0, tiled=True)]
    dot_general x6 -> x0, matrix products: 20 us -> none  [the longest x3 11.8 us: exact_dot(): jnp.dot(left, right, precision=lax.Precision.HIGHEST, preferred_element_t...]
    reduce_sum x6 -> x0, other arithmetic: 7.58 us -> none  [the longest x2 4.95 us: summed_on_arrival(): return jnp.sum(parts, axis=0)]
    broadcast_in_dim x2 -> x0, local copies, waits for them, and re-layouts: 3.57 us -> none  [copy_for_each(): jnp.broadcast_to(shard[None], (count, *shard.shape))]
    all_to_all x4 -> x0, local copies, waits for them, and re-layouts: 2.92 us -> none  [the longest x3 2.47 us: body(): lax.all_to_all(window_grads, 'row', split_axis=1, concat_axis=0, tiled=True)]
  transfers between devices with their start and end apart: 4 -> 0, of which waited for: 4 -> 0; matrix products, arithmetic and copies ran while one was open for 8% -> 0% of each run, Pallas kernels for 0% -> 0%
where the time goes in v1:
time: 54.8 us; the launch traced here: 54.6 us
  Pallas kernels  53.4 us (97%)
  local copies, waits for them, and re-layouts  1.26 us (2%)
    pallas_call x1, Pallas kernels, body(): pl.pallas_call(kernel, out_shape=jax.ShapeDtypeStruct((2, 256), f32), in_...  53.4 us
    unnamed x1, local copies, waits for them, and re-layouts  1.26 us

profile of v1, /device:TPU:1, one launch (start us, length us, event | category | flops | bytes accessed | tf_op | source)
XLA Modules:
  0.0 54.6 jit_solution(12458874660912450219)
XLA Ops:
  0.0 53.4 %shard_map.82 = f32[2,256]{1,0:T(2,128)} custom-call(f32[4096,512]{1,0:T(8,128)} %f_ref.1, f32[512,256]{1,0:T(8,128)} %q_ref.1, bf16[256,14336]{1,0:T(8,128)(2,1)} %h_ref.1, bf16[14336,128]{1,0:T(8,128)(2,1)} %pi_ref.1, bf16[256,4096]{1,0:T(8,128)(2,1)} %g_ref.1, bf16[4096,128]{1,0:T(8,128)(2,1)} %po_ref.1, s32[1,256]{1,0:T(1,128)} %bitcast.3, ...), custom_call_target="tpu_custom_call" | custom-call | tf_op jit(solution)/shard_map/pallas_call | solution.py:355
  53.4 1.3 %copy.10 = f32[2,256]{1,0:T(2,128)} copy(f32[2,256]{1,0:T(2,128)} %shard_map.82) | data formatting | bytes 4096

commit v2 on v1

--- a/solution.py
+++ b/solution.py
@@ -1,5 +1,3 @@
-import functools
-
 import jax
 import jax.numpy as jnp
 from jax import lax
@@ -12,6 +10,19 @@
 WIN = 17
 PITCH = 24
 KCH = 2048
+GROUPS = (
+    ((2, 0), (2, 1), (2, 2), (2, 3)),
+    ((1, 2), (3, 2), (0, 2), (1, 1)),
+    ((1, 3), (1, 0), (3, 1), (0, 1)),
+    ((3, 3), (3, 0), (0, 3), (0, 0)),
+)
+PEERS = sorted(
+    ((i // 16, i // 4 % 4, i % 4) for i in range(1, 64)),
+    key=lambda o: -sum(min(v, 4 - v) for v in o),
+)
+PLANE = ((2, 2), (2, 1), (1, 2), (2, 3), (3, 2), (1, 1), (1, 3), (3, 1), (3, 3),
+         (0, 2), (2, 0), (0, 1), (1, 0), (0, 3), (3, 0), (0, 0))
+TURNS = (2, 1, 3, 0)
 score_scale = 0.0625
 f32 = jnp.float32
 bf16 = jnp.bfloat16
@@ -30,13 +41,13 @@
 def kernel(
     f_ref, q_ref, h_ref, pi_ref, g_ref, po_ref, off_ref, len_ref, lens_ref,
     out_ref,
-    fv, qv, hv, piv, gv, pov, q3,
-    ua, ub, ca, cb,
+    fv, qv, hv, piv, gv, pov, q3, fs,
+    uu, cc, ua, ub,
     fa1, fb1, na1, nb1, fa2, fb2, na2, nb2,
     pt, pg, pgt, gsend, grecv, oneh, sbuf, srecv, sown, spart,
     fsem, qsem, hsem, gsem,
     csend, crecv, r_send, r_recv,
-    psend, precv, gssem, grsem, sssem, srsem, xsend, xrecv,
+    plane_sem, all_sem, psend, precv, gssem, grsem, sssem, srsem, xsend, xrecv,
 ):
     y = lax.axis_index("row")
     z = lax.axis_index("col_0")
@@ -56,95 +67,94 @@
     zp = (y, lax.rem(z + 1, 4), x, k)
     zm = (y, lax.rem(z + 3, 4), x, k)
 
-    grecv[...] = jnp.zeros_like(grecv)
-
-    barrier = pltpu.get_barrier_semaphore()
-
-    @pl.loop(1, 128)
-    def _(o):
-        pl.semaphore_signal(
-            barrier, inc=1,
-            device_id=(
-                lax.rem(y + o // 32, 4),
-                lax.rem(z + (o // 8) % 4, 4),
-                lax.rem(x + (o // 2) % 4, 4),
-                lax.rem(k + o % 2, 2),
-            ),
-            device_id_type=pl.DeviceIdType.MESH,
-        )
+    xs = [x] + [lax.rem(x + i, 4) for i in (1, 2, 3)]
+    zs = [z] + [lax.rem(z + i, 4) for i in (1, 2, 3)]
+    ys = [y] + [lax.rem(y + i, 4) for i in (1, 2, 3)]
+    ks = [k, lax.rem(k + 1, 2)]
 
     qcopy = pltpu.make_async_copy(q_ref, qv, qsem.at[0])
     qcopy.start()
-
-    def fcopy(g, dz):
-        dk = 1 - g // 4
-        dx = (6 - g % 4) % 4
-        a = lax.rem(k + dk, 2) * 16 + lax.rem(x + dx, 4) * 4 + lax.rem(z + dz, 4)
-        rows = pl.ds(pl.multiple_of(a * 128, 128), 128)
-        return pltpu.make_async_copy(f_ref.at[rows], fv.at[g, dz], fsem.at[g, dz])
-
-    @pl.loop(0, 32)
-    def _(i):
-        fcopy(i // 4, i % 4).start()
+    fcopies = {}
+    for n, group in enumerate(GROUPS):
+        for dk in (1, 0):
+            for i, (dx, dz) in enumerate(group):
+                a = ks[dk] * 16 + xs[dx] * 4 + zs[dz]
+                rows = pl.ds(pl.multiple_of(a * 128, 128), 128)
+                fcopies[n, dk, i] = pltpu.make_async_copy(
+                    f_ref.at[rows], fv.at[n * 2 + dk, i], fsem.at[n * 2 + dk, i]
+                )
+    for i in range(4):
+        fcopies[0, 1, i].start()
+
+    grecv[...] = jnp.zeros_like(grecv)
+
+    barrier = pltpu.get_barrier_semaphore()
+
+    def greet(sem, dev):
+        pl.semaphore_signal(sem, inc=1, device_id=dev, device_id_type=pl.DeviceIdType.MESH)
+
+    greet(barrier, partner)
+    for i in (1, 3, 2):
+        greet(barrier, (y, z, xs[i], k))
+        greet(barrier, (y, zs[i], x, k))
+        greet(barrier, (ys[i], z, x, k))
 
     def hcopies(c):
-        cols = pl.ds(pl.multiple_of(c * KCH, KCH), KCH)
+        cols = pl.ds(c * KCH, KCH)
         return (
             pltpu.make_async_copy(h_ref.at[:, cols], hv.at[c], hsem.at[0, c]),
             pltpu.make_async_copy(pi_ref.at[cols], piv.at[c], hsem.at[1, c]),
         )
 
     def gcopies(c):
-        cols = pl.ds(pl.multiple_of(c * KCH, KCH), KCH)
+        cols = pl.ds(c * KCH, KCH)
         return (
             pltpu.make_async_copy(g_ref.at[:, cols], gv.at[c], gsem.at[0, c]),
             pltpu.make_async_copy(po_ref.at[cols], pov.at[c], gsem.at[1, c]),
         )
 
-    @pl.loop(0, 2)
-    def _(c):
+    qcopy.wait()
+    for key, cp in fcopies.items():
+        if key[:2] != (0, 1):
+            cp.start()
+    for c in range(2):
         for cp in gcopies(c):
             cp.start()
-
-    @pl.loop(0, 7)
-    def _(c):
+    for c in range(7):
         for cp in hcopies(c):
             cp.start()
-
-    qcopy.wait()
     qh, ql = split(qv[...])
     q3[0:512] = qh
     q3[512:1024] = ql
     q3[1024:1536] = qh
 
-    @pl.loop(0, 8)
-    def _(g):
-        for dz in range(4):
-            fcopy(g, dz).wait()
-        dk = 1 - g // 4
-        dx = (6 - g % 4) % 4
-        hi, lo = split(fv[g].reshape(512, 512))
-        u = dot(jnp.concatenate([hi, hi, lo], axis=1), q3[...]).reshape(4, 128, 256)
-        ua[dk, dx] = u[:, 0:64]
-        for dz in range(4):
-            ub[dk, dz, dx] = u[dz, 64:128]
-
-    pl.semaphore_wait(barrier, 127)
-
-    order = (2, 1, 3, 0)
+    def prepare(n, dk):
+        for i in range(4):
+            fcopies[n, dk, i].wait()
+        hi, lo = split(fv[n * 2 + dk].reshape(512, 512))
+        fs[dk, 0] = hi
+        fs[dk, 1] = lo
+
+    def compute(n, dk):
+        for i in range(2):
+            hi, lo = (fs[dk, j, i * 256 : i * 256 + 256] for j in range(2))
+            v = dot(jnp.concatenate([hi, hi, lo], axis=1), q3[...])
+            uu[dk, n, i * 2 : i * 2 + 2] = v.reshape(2, 128, 256)
+
+    done = []
     swaps = {}
-    for n, q in enumerate(order):
-        for c, (u, r) in enumerate(((ua, ca), (ub, cb))):
-            cp = remote(u.at[1, q], r.at[q], csend.at[c, q], crecv.at[c, q], partner)
-            cp.start()
-            swaps[c, q] = cp
-
-    done = list(swaps.values())
-
-    def merge(c, q):
-        u, r = ((ua, ca), (ub, cb))[c]
-        swaps[c, q].wait_recv()
-        u[0, q] = u[0, q] + r[q]
+
+    def swap(n):
+        swaps[n] = remote(uu.at[1, n], cc.at[n], csend.at[n], crecv.at[n], partner)
+        swaps[n].start()
+        done.append(swaps[n])
+
+    def merge(n):
+        swaps[n].wait_recv()
+        for i, (dx, dz) in enumerate(GROUPS[n]):
+            v = uu[0, n, i] + cc[n, i]
+            ua[dx, dz] = v[0:64]
+            ub[dz, dx] = v[64:128]
 
     class Ring:
         def __init__(self, p, half, far, near, ids, plus, minus):
@@ -189,50 +199,69 @@
                 self.recv[name].wait_recv()
             self.p[0] = self.p[0] + self.near[0] + self.near[1]
 
-    ring_a = Ring(ua.at[0], 2, fa1, na1, 0, xp, xm)
-    ring_b = Ring(ub.at[0], 2, fb1, nb1, 1, zp, zm)
-    ring_a2 = Ring(ua.at[0, 0], 32, fa2, na2, 2, zp, zm)
-    ring_b2 = Ring(ub.at[0, 0], 32, fb2, nb2, 3, xp, xm)
-
-    merge(0, 2)
+    ring_a = Ring(ua, 2, fa1, na1, 0, xp, xm)
+    ring_b = Ring(ub, 2, fb1, nb1, 1, zp, zm)
+    ring_a2 = Ring(ua.at[0], 32, fa2, na2, 2, zp, zm)
+    ring_b2 = Ring(ub.at[0], 32, fb2, nb2, 3, xp, xm)
+
+    prepare(0, 1)
+    prepare(0, 0)
+    compute(0, 1)
+    pl.semaphore_wait(barrier, 10)
+    for i in (1, 3, 2):
+        greet(plane_sem, (y, zs[i], x, k))
+    swap(0)
+    prepare(1, 1)
+    compute(0, 0)
+    prepare(1, 0)
+    compute(1, 1)
+    swap(1)
+    merge(0)
     ring_a.send_far()
-    merge(1, 2)
+    prepare(2, 1)
+    compute(1, 0)
+    prepare(2, 0)
+    compute(2, 1)
+    swap(2)
+    merge(1)
     ring_b.send_far()
-    merge(0, 1)
+    prepare(3, 1)
+    compute(2, 0)
+    prepare(3, 0)
+    compute(3, 1)
+    swap(3)
+    merge(2)
     ring_a.send_plus_early()
-    merge(1, 1)
     ring_b.send_plus_early()
-    merge(0, 3)
+    compute(3, 0)
+    pl.semaphore_wait(plane_sem, 3)
+    for i in (1, 3, 2):
+        greet(all_sem, (ys[i], z, x, k))
+    merge(3)
     ring_a.send_minus_early()
-    merge(1, 3)
     ring_b.send_minus_early()
-    merge(0, 0)
-    merge(1, 0)
 
     mine = pl.ds(pl.multiple_of(k * 256, 256), 256)
-    pg[mine] = jnp.zeros((256, 128), f32)
-    pt[mine] = jnp.zeros((256, 128), f32)
-
-    @pl.loop(0, 2)
-    def _(c):
-        for cp in gcopies(c):
-            cp.wait()
-        pg[mine] = pg[mine] + dot(gv[c], pov[c])
-
-    @pl.loop(0, 7)
-    def _(c):
-        for cp in hcopies(c):
-            cp.wait()
-        pt[mine] = pt[mine] + dot(hv[c], piv[c])
+
+    def proj(store, copies, a, b, cs):
+        for c in cs:
+            for cp in copies(c):
+                cp.wait()
+            v = dot(a[c], b[c])
+            store[mine] = v if c == 0 else store[mine] + v
+
+    proj(pg, gcopies, gv, pov, range(2))
+    proj(pt, hcopies, hv, piv, range(1))
+    ring_a.relay()
+    proj(pt, hcopies, hv, piv, range(1, 4))
+    ring_b.relay()
+    proj(pt, hcopies, hv, piv, range(4, 7))
 
     give_g = remote(pg.at[mine], pg.at[mine], psend.at[0], precv.at[0], partner)
     give_t = remote(pt.at[mine], pt.at[mine], psend.at[1], precv.at[1], partner)
     give_g.start()
     give_t.start()
     done.extend((give_g, give_t))
-
-    ring_a.relay()
-    ring_b.relay()
 
     off_row = off_ref[...].astype(f32)
     end_row = off_row + len_ref[...].astype(f32)
@@ -253,40 +282,54 @@
     pgt[...] = jnp.transpose(pg[...]).reshape(8, 16, 512)
     th, tl = split(pt[...])
     t3 = jnp.concatenate([th, tl, th], axis=0)
-    for yy in range(4):
-        lines = pgt[yy * 2 + k]
-        spread = (lines[:, None, :] * member[None, :, :]).reshape(16 * PITCH, 512)
+    for half in range(2):
+        lines = jnp.concatenate([pgt[half * 4 + k], pgt[half * 4 + 2 + k]], axis=0)
+        spread = (lines[:, None, :] * member[None, :, :]).reshape(32 * PITCH, 512)
         hi, lo = split(spread)
-        grads = dot(jnp.concatenate([hi, hi, lo], axis=1), t3)
-        gsend[yy * 16 : yy * 16 + 16] = grads.reshape(16, PITCH, 128)
-
-    def peer(o):
-        return (
-            lax.rem(y + o // 16, 4),
-            lax.rem(z + o % 4, 4),
-            lax.rem(x + (o // 4) % 4, 4),
-        )
-
-    @pl.loop(1, 64)
-    def _(o):
-        py, pz, px = peer(o)
-        remote(
-            gsend.at[py * 16 + px * 4 + pz, pl.ds(0, WIN)],
-            grecv.at[chip, pl.ds(0, WIN)],
-            gssem.at[0], grsem.at[0], (py, pz, px, k),
-        ).start()
-
-    grecv[chip] = gsend[y * 16 + x * 4 + z]
+        rows = jnp.concatenate([hi, hi, lo], axis=1)
+        grads = jnp.concatenate([dot(rows[i : i + 256], t3) for i in (0, 256, 512)], axis=0)
+        gsend[half * 32 : half * 32 + 32] = grads.reshape(32, PITCH, 128)
+
+    pl.semaphore_wait(all_sem, 3)
+
+    def spread_grads(p):
+        oy = TURNS[p]
+        for oz, ox in PLANE:
+            if (oy, oz, ox) != (0, 0, 0):
+                remote(
+                    gsend.at[ys[oy] * 16 + xs[ox] * 4 + zs[oz], pl.ds(0, WIN)],
+                    grecv.at[p * 16 + oz * 4 + ox, pl.ds(0, WIN)],
+                    gssem.at[0], grsem.at[p], (ys[oy], zs[oz], xs[ox], k),
+                ).start()
+
+    spread_grads(0)
+    grecv[48] = gsend[y * 16 + x * 4 + z]
 
     cols = lax.broadcasted_iota(jnp.int32, (1, 64 * PITCH), 1)
-    col_chip = (cols * 2731) >> 16
-    col_win = cols - col_chip * PITCH
+    place = (cols * 2731) >> 16
+    col_win = cols - place * PITCH
+    turn = place >> 4
+    from_y = y - jnp.where(turn == 0, 2, jnp.where(turn == 1, 1, jnp.where(turn == 2, 3, 0)))
+    from_z = z - ((place >> 2) & 3)
+    from_x = x - (place & 3)
+    col_chip = (from_y & 3) * 16 + (from_z & 3) * 4 + (from_x & 3)
     col_slot = (col_chip * 512).astype(f32)
     before = jnp.sum((end_col <= col_slot).astype(f32), axis=0, keepdims=True)
     target = jnp.where(col_win < WIN, before + col_win.astype(f32), -1.0)
     line = lax.broadcasted_iota(jnp.int32, (512, 1), 0)
     sample = (line >> 3) * 4 + ((line >> 2) & 1) * 2 + (line & 1)
     oneh[...] = (sample.astype(f32) == target).astype(f32).astype(bf16)
+
+    def gather_grads(first, count):
+        for p in range(first // 16, (first + count) // 16):
+            n = 15 if p == 3 else 16
+            slots = grecv.at[pl.ds(p * 16, n), pl.ds(0, WIN)]
+            pltpu.make_async_copy(slots, slots, grsem.at[p]).wait()
+        part = pl.ds(first * PITCH, count * PITCH)
+        gh, gl = split(grecv[first : first + count].reshape(count * PITCH, 128))
+        gg = jnp.concatenate([gh, gl], axis=0)
+        picks = (oneh[0:256, part], oneh[256:512, part])
+        return [dot(jnp.concatenate([m, m], axis=1), gg) for m in picks]
 
     ring_a.finish()
     ring_a2.send_far()
@@ -296,30 +339,30 @@
     ring_b2.send_far()
     ring_b2.send_plus_early()
     ring_b2.send_minus_early()
+    spread_grads(1)
+    spread_grads(2)
     ring_a2.relay()
     ring_b2.relay()
+    spread_grads(3)
     ring_a2.finish()
     ring_b2.finish()
-
-    uh, ul = split(jnp.concatenate([ua[0, 0, 0], ub[0, 0, 0]], axis=0))
+    dense_a = gather_grads(0, 32)
+
+    uh, ul = split(jnp.concatenate([ua[0, 0], ub[0, 0]], axis=0))
     u3 = jnp.concatenate([uh, ul, uh], axis=0)
 
-    pltpu.make_async_copy(
-        grecv.at[pl.ds(0, 63), pl.ds(0, WIN)], grecv.at[pl.ds(0, 63), pl.ds(0, WIN)], grsem.at[0]
-    ).wait()
-    gh, gl = split(grecv[...].reshape(64 * PITCH, 128))
-    dense = dot(oneh[...], gh) + dot(oneh[...], gl)
-    dh, dl = split(dense)
-    both = dot(jnp.concatenate([dh, dh, dl], axis=1), u3)
-    upper = ((line >> 1) & 1) == 0
-    sbuf[...] = jnp.where(upper, both[:, 0:128], both[:, 128:256]).reshape(64, 8, 128)
-
-    @pl.loop(1, 64)
-    def _(o):
-        py, pz, px = peer(o)
+    dense_b = gather_grads(32, 32)
+    upper = ((line[0:256] >> 1) & 1) == 0
+    for i in range(2):
+        dh, dl = split(dense_a[i] + dense_b[i])
+        both = dot(jnp.concatenate([dh, dh, dl], axis=1), u3)
+        tiles = jnp.where(upper, both[:, 0:128], both[:, 128:256])
+        sbuf[i * 32 : i * 32 + 32] = tiles.reshape(32, 8, 128)
+
+    for oy, oz, ox in PEERS:
         remote(
-            sbuf.at[py * 16 + pz * 4 + px], srecv.at[chip],
-            sssem.at[0], srsem.at[0], (py, pz, px, k),
+            sbuf.at[ys[oy] * 16 + zs[oz] * 4 + xs[ox]], srecv.at[chip],
+            sssem.at[0], srsem.at[0], (ys[oy], zs[oz], xs[ox], k),
         ).start()
 
     srecv[chip] = sbuf[chip]
@@ -361,8 +404,8 @@
             vmem((8, 4, 128, 512), f32), vmem((512, 256), f32),
             vmem((7, 256, KCH), bf16), vmem((7, KCH, 128), bf16),
             vmem((2, 256, KCH), bf16), vmem((2, KCH, 128), bf16),
-            vmem((1536, 256), bf16),
-            vmem((2, 4, 4, 64, 256), f32), vmem((2, 4, 4, 64, 256), f32),
+            vmem((1536, 256), bf16), vmem((2, 2, 512, 512), bf16),
+            vmem((2, 4, 4, 128, 256), f32), vmem((4, 4, 128, 256), f32),
             vmem((4, 4, 64, 256), f32), vmem((4, 4, 64, 256), f32),
             vmem((2, 2, 64, 256), f32), vmem((2, 2, 64, 256), f32),
             vmem((2, 4, 64, 256), f32), vmem((2, 4, 64, 256), f32),
@@ -374,8 +417,9 @@
             vmem((64, 8, 128), f32), vmem((64, 8, 128), f32),
             vmem((8, 128), f32), vmem((8, 128), f32),
             dma((8, 4)), dma((1,)), dma((2, 7)), dma((2, 2)),
-            dma((2, 4)), dma((2, 4)), dma((4, 6)), dma((4, 6)),
-            dma((2,)), dma((2,)), dma((1,)), dma((1,)), dma((1,)), dma((1,)),
+            dma((4,)), dma((4,)), dma((4, 6)), dma((4, 6)),
+            pltpu.SemaphoreType.REGULAR, pltpu.SemaphoreType.REGULAR,
+            dma((2,)), dma((2,)), dma((1,)), dma((4,)), dma((1,)), dma((1,)),
             dma((1,)), dma((1,)),
         ],
         compiler_params=pltpu.CompilerParams(

time: 54.8 us -> 48.9 us (0.89)
  Pallas kernels: 53.4 us -> 47.5 us
    pallas_call x1, Pallas kernels: 53.4 us -> 47.5 us  [body(): pl.pallas_call(kernel, out_shape=jax.ShapeDtypeStruct((2, 256), f32), in_...]
where the time goes in v2:
time: 48.9 us; the launch traced here: 48.8 us
  Pallas kernels  47.5 us (97%)
  local copies, waits for them, and re-layouts  1.26 us (3%)
    pallas_call x1, Pallas kernels, body(): pl.pallas_call(kernel, out_shape=jax.ShapeDtypeStruct((2, 256), f32), in_...  47.5 us
    unnamed x1, local copies, waits for them, and re-layouts  1.26 us

profile of v2, /device:TPU:1, one launch (start us, length us, event | category | flops | bytes accessed | tf_op | source)
XLA Modules:
  0.0 48.8 jit_solution(4404904791944177763)
XLA Ops:
  0.0 47.5 %shard_map.82 = f32[2,256]{1,0:T(2,128)} custom-call(f32[4096,512]{1,0:T(8,128)} %f_ref.1, f32[512,256]{1,0:T(8,128)} %q_ref.1, bf16[256,14336]{1,0:T(8,128)(2,1)} %h_ref.1, bf16[14336,128]{1,0:T(8,128)(2,1)} %pi_ref.1, bf16[256,4096]{1,0:T(8,128)(2,1)} %g_ref.1, bf16[4096,128]{1,0:T(8,128)(2,1)} %po_ref.1, s32[1,256]{1,0:T(1,128)} %bitcast.3, ...), custom_call_target="tpu_custom_call" | custom-call | tf_op jit(solution)/shard_map/pallas_call | solution.py:398
  47.5 1.3 %copy.10 = f32[2,256]{1,0:T(2,128)} copy(f32[2,256]{1,0:T(2,128)} %shard_map.82) | data formatting | bytes 4096

commit v3 on v2

--- a/solution.py
+++ b/solution.py
@@ -12,9 +12,9 @@
 KCH = 2048
 GROUPS = (
     ((2, 0), (2, 1), (2, 2), (2, 3)),
-    ((1, 2), (3, 2), (0, 2), (1, 1)),
-    ((1, 3), (1, 0), (3, 1), (0, 1)),
-    ((3, 3), (3, 0), (0, 3), (0, 0)),
+    ((1, 2), (3, 2), (0, 2), (1, 3)),
+    ((3, 0), (3, 1), (0, 3), (1, 1)),
+    ((1, 0), (3, 3), (0, 1), (0, 0)),
 )
 PEERS = sorted(
     ((i // 16, i // 4 % 4, i % 4) for i in range(1, 64)),
@@ -41,13 +41,13 @@
 def kernel(
     f_ref, q_ref, h_ref, pi_ref, g_ref, po_ref, off_ref, len_ref, lens_ref,
     out_ref,
-    fv, qv, hv, piv, gv, pov, q3, fs,
+    fv, qv, hv, piv, gv, pov, q3,
     uu, cc, ua, ub,
     fa1, fb1, na1, nb1, fa2, fb2, na2, nb2,
-    pt, pg, pgt, gsend, grecv, oneh, sbuf, srecv, sown, spart,
+    pt, pg, pgt, gsend, grecv, oneh, sbuf, srecv, other,
     fsem, qsem, hsem, gsem,
     csend, crecv, r_send, r_recv,
-    plane_sem, all_sem, psend, precv, gssem, grsem, sssem, srsem, xsend, xrecv,
+    plane_sem, all_sem, psend, precv, gssem, grsem, sssem, srsem, xsend,
 ):
     y = lax.axis_index("row")
     z = lax.axis_index("col_0")
@@ -83,8 +83,9 @@
                 fcopies[n, dk, i] = pltpu.make_async_copy(
                     f_ref.at[rows], fv.at[n * 2 + dk, i], fsem.at[n * 2 + dk, i]
                 )
-    for i in range(4):
-        fcopies[0, 1, i].start()
+    for dk in (1, 0):
+        for i in range(4):
+            fcopies[0, dk, i].start()
 
     grecv[...] = jnp.zeros_like(grecv)
 
@@ -100,14 +101,14 @@
         greet(barrier, (ys[i], z, x, k))
 
     def hcopies(c):
-        cols = pl.ds(c * KCH, KCH)
+        cols = pl.ds(pl.multiple_of(c * KCH, KCH), KCH)
         return (
             pltpu.make_async_copy(h_ref.at[:, cols], hv.at[c], hsem.at[0, c]),
             pltpu.make_async_copy(pi_ref.at[cols], piv.at[c], hsem.at[1, c]),
         )
 
     def gcopies(c):
-        cols = pl.ds(c * KCH, KCH)
+        cols = pl.ds(pl.multiple_of(c * KCH, KCH), KCH)
         return (
             pltpu.make_async_copy(g_ref.at[:, cols], gv.at[c], gsem.at[0, c]),
             pltpu.make_async_copy(po_ref.at[cols], pov.at[c], gsem.at[1, c]),
@@ -115,7 +116,7 @@
 
     qcopy.wait()
     for key, cp in fcopies.items():
-        if key[:2] != (0, 1):
+        if key[0]:
             cp.start()
     for c in range(2):
         for cp in gcopies(c):
@@ -128,18 +129,16 @@
     q3[512:1024] = ql
     q3[1024:1536] = qh
 
-    def prepare(n, dk):
+    def compute(n, dk):
         for i in range(4):
             fcopies[n, dk, i].wait()
-        hi, lo = split(fv[n * 2 + dk].reshape(512, 512))
-        fs[dk, 0] = hi
-        fs[dk, 1] = lo
-
-    def compute(n, dk):
-        for i in range(2):
-            hi, lo = (fs[dk, j, i * 256 : i * 256 + 256] for j in range(2))
+
+        @pl.loop(0, 2)
+        def _(i):
+            pair = pl.ds(i * 2, 2)
+            hi, lo = split(fv[n * 2 + dk, pair].reshape(256, 512))
             v = dot(jnp.concatenate([hi, hi, lo], axis=1), q3[...])
-            uu[dk, n, i * 2 : i * 2 + 2] = v.reshape(2, 128, 256)
+            uu[dk, n, pair] = v.reshape(2, 128, 256)
 
     done = []
     swaps = {}
@@ -204,62 +203,55 @@
     ring_a2 = Ring(ua.at[0], 32, fa2, na2, 2, zp, zm)
     ring_b2 = Ring(ub.at[0], 32, fb2, nb2, 3, xp, xm)
 
-    prepare(0, 1)
-    prepare(0, 0)
     compute(0, 1)
     pl.semaphore_wait(barrier, 10)
     for i in (1, 3, 2):
         greet(plane_sem, (y, zs[i], x, k))
     swap(0)
-    prepare(1, 1)
     compute(0, 0)
-    prepare(1, 0)
     compute(1, 1)
     swap(1)
     merge(0)
     ring_a.send_far()
-    prepare(2, 1)
     compute(1, 0)
-    prepare(2, 0)
     compute(2, 1)
     swap(2)
     merge(1)
     ring_b.send_far()
-    prepare(3, 1)
     compute(2, 0)
-    prepare(3, 0)
     compute(3, 1)
     swap(3)
     merge(2)
     ring_a.send_plus_early()
+    ring_a.send_minus_early()
     ring_b.send_plus_early()
+    ring_b.send_minus_early()
     compute(3, 0)
     pl.semaphore_wait(plane_sem, 3)
     for i in (1, 3, 2):
         greet(all_sem, (ys[i], z, x, k))
-    merge(3)
-    ring_a.send_minus_early()
-    ring_b.send_minus_early()
 
     mine = pl.ds(pl.multiple_of(k * 256, 256), 256)
-
-    def proj(store, copies, a, b, cs):
-        for c in cs:
+    pg[mine] = jnp.zeros((256, 128), f32)
+    pt[mine] = jnp.zeros((256, 128), f32)
+
+    def proj(store, copies, a, b, first, end):
+        @pl.loop(first, end)
+        def _(c):
             for cp in copies(c):
                 cp.wait()
-            v = dot(a[c], b[c])
-            store[mine] = v if c == 0 else store[mine] + v
-
-    proj(pg, gcopies, gv, pov, range(2))
-    proj(pt, hcopies, hv, piv, range(1))
+            store[mine] = store[mine] + dot(a[c], b[c])
+
+    proj(pg, gcopies, gv, pov, 0, 2)
+    give_g = remote(pg.at[mine], pg.at[mine], psend.at[0], precv.at[0], partner)
+    give_g.start()
+    merge(3)
+    proj(pt, hcopies, hv, piv, 0, 2)
     ring_a.relay()
-    proj(pt, hcopies, hv, piv, range(1, 4))
+    proj(pt, hcopies, hv, piv, 2, 4)
     ring_b.relay()
-    proj(pt, hcopies, hv, piv, range(4, 7))
-
-    give_g = remote(pg.at[mine], pg.at[mine], psend.at[0], precv.at[0], partner)
+    proj(pt, hcopies, hv, piv, 4, 7)
     give_t = remote(pt.at[mine], pt.at[mine], psend.at[1], precv.at[1], partner)
-    give_g.start()
     give_t.start()
     done.extend((give_g, give_t))
 
@@ -281,15 +273,28 @@
     give_t.wait_recv()
     pgt[...] = jnp.transpose(pg[...]).reshape(8, 16, 512)
     th, tl = split(pt[...])
-    t3 = jnp.concatenate([th, tl, th], axis=0)
-    for half in range(2):
+    t2 = jnp.concatenate([th, tl], axis=1)
+
+    def window_grads(half):
         lines = jnp.concatenate([pgt[half * 4 + k], pgt[half * 4 + 2 + k]], axis=0)
         spread = (lines[:, None, :] * member[None, :, :]).reshape(32 * PITCH, 512)
         hi, lo = split(spread)
-        rows = jnp.concatenate([hi, hi, lo], axis=1)
-        grads = jnp.concatenate([dot(rows[i : i + 256], t3) for i in (0, 256, 512)], axis=0)
-        gsend[half * 32 : half * 32 + 32] = grads.reshape(32, PITCH, 128)
-
+        grads = []
+        for i in (0, 256, 512):
+            v = dot(hi[i : i + 256], t2)
+            grads.append(v[:, 0:128] + v[:, 128:256] + dot(lo[i : i + 256], th))
+        gsend[pl.ds(half * 32, 32)] = jnp.concatenate(grads, axis=0).reshape(32, PITCH, 128)
+
+    window_grads(0)
+    ring_a.finish()
+    ring_a2.send_far()
+    ring_a2.send_plus_early()
+    ring_a2.send_minus_early()
+    ring_b.finish()
+    ring_b2.send_far()
+    ring_b2.send_plus_early()
+    ring_b2.send_minus_early()
+    window_grads(1)
     pl.semaphore_wait(all_sem, 3)
 
     def spread_grads(p):
@@ -302,8 +307,11 @@
                     gssem.at[0], grsem.at[p], (ys[oy], zs[oz], xs[ox], k),
                 ).start()
 
-    spread_grads(0)
+    for p in range(4):
+        spread_grads(p)
     grecv[48] = gsend[y * 16 + x * 4 + z]
+    ring_a2.relay()
+    ring_b2.relay()
 
     cols = lax.broadcasted_iota(jnp.int32, (1, 64 * PITCH), 1)
     place = (cols * 2731) >> 16
@@ -327,23 +335,10 @@
             pltpu.make_async_copy(slots, slots, grsem.at[p]).wait()
         part = pl.ds(first * PITCH, count * PITCH)
         gh, gl = split(grecv[first : first + count].reshape(count * PITCH, 128))
-        gg = jnp.concatenate([gh, gl], axis=0)
-        picks = (oneh[0:256, part], oneh[256:512, part])
-        return [dot(jnp.concatenate([m, m], axis=1), gg) for m in picks]
-
-    ring_a.finish()
-    ring_a2.send_far()
-    ring_a2.send_plus_early()
-    ring_a2.send_minus_early()
-    ring_b.finish()
-    ring_b2.send_far()
-    ring_b2.send_plus_early()
-    ring_b2.send_minus_early()
-    spread_grads(1)
-    spread_grads(2)
-    ring_a2.relay()
-    ring_b2.relay()
-    spread_grads(3)
+        gg = jnp.concatenate([gh, gl], axis=1)
+        both = [dot(oneh[i : i + 256, part], gg) for i in (0, 256)]
+        return [v[:, 0:128] + v[:, 128:256] for v in both]
+
     ring_a2.finish()
     ring_b2.finish()
     dense_a = gather_grads(0, 32)
@@ -360,34 +355,39 @@
         sbuf[i * 32 : i * 32 + 32] = tiles.reshape(32, 8, 128)
 
     for oy, oz, ox in PEERS:
-        remote(
-            sbuf.at[ys[oy] * 16 + zs[oz] * 4 + xs[ox]], srecv.at[chip],
-            sssem.at[0], srsem.at[0], (ys[oy], zs[oz], xs[ox], k),
-        ).start()
-
-    srecv[chip] = sbuf[chip]
-    pltpu.make_async_copy(
-        srecv.at[pl.ds(0, 63)], srecv.at[pl.ds(0, 63)], srsem.at[0]
-    ).wait()
-    sown[...] = jnp.sum(srecv[...], axis=0)
-    last = remote(sown, spart, xsend.at[0], xrecv.at[0], partner)
+        for kk in range(2):
+            remote(
+                sbuf.at[ys[oy] * 16 + zs[oz] * 4 + xs[ox], pl.ds(kk * 4, 4)],
+                srecv.at[k * 64 + chip, pl.ds(0, 4)],
+                sssem.at[0], srsem.at[0], (ys[oy], zs[oz], xs[ox], kk),
+            ).start()
+    own = sbuf[chip]
+    srecv[k * 64 + chip, 0:4] = jnp.where(k == 0, own[0:4], own[4:8])
+    other[0:4] = jnp.where(k == 0, own[4:8], own[0:4])
+    last = remote(
+        other.at[pl.ds(0, 4)], srecv.at[k * 64 + chip, pl.ds(0, 4)],
+        xsend.at[0], xsend.at[1], partner,
+    )
     last.start()
+    done.append(last)
+
+    slots = srecv.at[pl.ds(0, 126), pl.ds(0, 4)]
+    pltpu.make_async_copy(slots, slots, srsem.at[0]).wait()
     last.wait_recv()
-    tile = sown[...] + spart[...]
-    tile = jnp.where(k == 0, tile[0:4], tile[4:8]) * score_scale
+    tile = jnp.sum(srecv[:, 0:4], axis=0)
     d = chip * 2 + k
     for s in range(2):
         n = lens_ref[2 * d + s].astype(f32)
         for j in range(2):
-            out_ref[s : s + 1, j * 128 : j * 128 + 128] = tile[j * 2 + s : j * 2 + s + 1] / n
-
-    last.wait_send()
+            line = tile[j * 2 + s : j * 2 + s + 1] * score_scale
+            out_ref[s : s + 1, j * 128 : j * 128 + 128] = line / n
+
     for cp in done:
         cp.wait_send()
-    pltpu.make_async_copy(
-        gsend.at[pl.ds(0, 63), pl.ds(0, WIN)], gsend.at[pl.ds(0, 63), pl.ds(0, WIN)], gssem.at[0]
-    ).wait()
-    pltpu.make_async_copy(sbuf.at[pl.ds(0, 63)], sbuf.at[pl.ds(0, 63)], sssem.at[0]).wait()
+    sent = gsend.at[pl.ds(0, 63), pl.ds(0, WIN)]
+    pltpu.make_async_copy(sent, sent, gssem.at[0]).wait()
+    sent = sbuf.at[pl.ds(0, 63)]
+    pltpu.make_async_copy(sent, sent, sssem.at[0]).wait()
 
 
 def body(hidden_in, out_grad, proj_in, proj_out, inverse_fisher, queries, lengths, offsets):
@@ -397,14 +397,14 @@
     invm = pl.BlockSpec(memory_space=pltpu.VMEM)
     return pl.pallas_call(
         kernel,
-        out_shape=jax.ShapeDtypeStruct((2, 256), f32),
+        out_shape=pltpu.VMEM((2, 256), f32),
         in_specs=[anys] * 6 + [invm] * 2 + [pl.BlockSpec(memory_space=pltpu.SMEM)],
         out_specs=invm,
         scratch_shapes=[
             vmem((8, 4, 128, 512), f32), vmem((512, 256), f32),
             vmem((7, 256, KCH), bf16), vmem((7, KCH, 128), bf16),
             vmem((2, 256, KCH), bf16), vmem((2, KCH, 128), bf16),
-            vmem((1536, 256), bf16), vmem((2, 2, 512, 512), bf16),
+            vmem((1536, 256), bf16),
             vmem((2, 4, 4, 128, 256), f32), vmem((4, 4, 128, 256), f32),
             vmem((4, 4, 64, 256), f32), vmem((4, 4, 64, 256), f32),
             vmem((2, 2, 64, 256), f32), vmem((2, 2, 64, 256), f32),
@@ -414,13 +414,12 @@
             vmem((512, 128), f32), vmem((512, 128), f32), vmem((8, 16, 512), f32),
             vmem((64, PITCH, 128), f32), vmem((64, PITCH, 128), f32),
             vmem((512, 64 * PITCH), bf16),
-            vmem((64, 8, 128), f32), vmem((64, 8, 128), f32),
-            vmem((8, 128), f32), vmem((8, 128), f32),
+            vmem((64, 8, 128), f32), vmem((128, 8, 128), f32), vmem((8, 128), f32),
             dma((8, 4)), dma((1,)), dma((2, 7)), dma((2, 2)),
             dma((4,)), dma((4,)), dma((4, 6)), dma((4, 6)),
             pltpu.SemaphoreType.REGULAR, pltpu.SemaphoreType.REGULAR,
             dma((2,)), dma((2,)), dma((1,)), dma((4,)), dma((1,)), dma((1,)),
-            dma((1,)), dma((1,)),
+            dma((2,)),
         ],
         compiler_params=pltpu.CompilerParams(
             collective_id=0, has_side_effects=True, vmem_limit_bytes=60 * 1024 * 1024

time: 48.9 us -> 43 us (0.88)
  Pallas kernels: 47.5 us -> 42.2 us
  local copies, waits for them, and re-layouts: 1.26 us -> 0.58 us
    pallas_call x1, Pallas kernels: 47.5 us -> 42.2 us  [body(): pl.pallas_call(kernel, out_shape=pltpu.VMEM((2, 256), f32), in_specs=[any...]
    unnamed x1, local copies, waits for them, and re-layouts: 1.26 us -> 0.58 us
where the time goes in v3:
time: 43 us; the launch traced here: 42.8 us
  Pallas kernels  42.2 us (98%)
  local copies, waits for them, and re-layouts  0.58 us (1%)
    pallas_call x1, Pallas kernels, body(): pl.pallas_call(kernel, out_shape=pltpu.VMEM((2, 256), f32), in_specs=[any...  42.2 us

profile of v3, /device:TPU:1, one launch (start us, length us, event | category | flops | bytes accessed | tf_op | source)
XLA Modules:
  0.0 42.8 jit_solution(12920766610767534874)
XLA Ops:
  0.0 42.2 %shard_map.82 = f32[2,256]{1,0:T(2,128)S(1)} custom-call(f32[4096,512]{1,0:T(8,128)} %f_ref.1, f32[512,256]{1,0:T(8,128)} %q_ref.1, bf16[256,14336]{1,0:T(8,128)(2,1)} %h_ref.1, bf16[14336,128]{1,0:T(8,128)(2,1)} %pi_ref.1, bf16[256,4096]{1,0:T(8,128)(2,1)} %g_ref.1, bf16[4096,128]{1,0:T(8,128)(2,1)} %po_ref.1, s32[1,256]{1,0:T(1,128)} %bitcast.3, ...), custom_call_target="tpu_custom_call" | custom-call | tf_op jit(solution)/shard_map/pallas_call | solution.py:398
  42.3 0.6 %copy.10 = f32[2,256]{1,0:T(2,128)} copy(f32[2,256]{1,0:T(2,128)S(1)} %shard_map.82) | data formatting | bytes 4096

commit v4 on v3

--- a/solution.py
+++ b/solution.py
@@ -11,10 +11,8 @@
 PITCH = 24
 KCH = 2048
 GROUPS = (
-    ((2, 0), (2, 1), (2, 2), (2, 3)),
-    ((1, 2), (3, 2), (0, 2), (1, 3)),
-    ((3, 0), (3, 1), (0, 3), (1, 1)),
-    ((1, 0), (3, 3), (0, 1), (0, 0)),
+    ((2, 2), (2, 0)), ((0, 2), (2, 1)), ((2, 3), (3, 2)), ((1, 2), (1, 3)),
+    ((3, 0), (3, 1)), ((0, 3), (1, 1)), ((1, 0), (3, 3)), ((0, 1), (0, 0)),
 )
 PEERS = sorted(
     ((i // 16, i // 4 % 4, i % 4) for i in range(1, 64)),
@@ -39,13 +37,13 @@
 
 
 def kernel(
-    f_ref, q_ref, h_ref, pi_ref, g_ref, po_ref, off_ref, len_ref, lens_ref,
+    f_ref, q_ref, h_ref, pi_ref, g_ref, po_ref, off_hbm, len_hbm,
     out_ref,
     fv, qv, hv, piv, gv, pov, q3,
     uu, cc, ua, ub,
     fa1, fb1, na1, nb1, fa2, fb2, na2, nb2,
     pt, pg, pgt, gsend, grecv, oneh, sbuf, srecv, other,
-    fsem, qsem, hsem, gsem,
+    off_ref, len_ref, fsem, qsem, lsem, hsem, gsem,
     csend, crecv, r_send, r_recv,
     plane_sem, all_sem, psend, precv, gssem, grsem, sssem, srsem, xsend,
 ):
@@ -84,8 +82,15 @@
                     f_ref.at[rows], fv.at[n * 2 + dk, i], fsem.at[n * 2 + dk, i]
                 )
     for dk in (1, 0):
-        for i in range(4):
+        for i in range(2):
             fcopies[0, dk, i].start()
+
+    lcopies = (
+        pltpu.make_async_copy(off_hbm, off_ref, lsem.at[0]),
+        pltpu.make_async_copy(len_hbm, len_ref, lsem.at[1]),
+    )
+    for cp in lcopies:
+        cp.start()
 
     grecv[...] = jnp.zeros_like(grecv)
 
@@ -130,15 +135,14 @@
     q3[1024:1536] = qh
 
     def compute(n, dk):
-        for i in range(4):
+        for i in range(2):
             fcopies[n, dk, i].wait()
 
-        @pl.loop(0, 2)
-        def _(i):
-            pair = pl.ds(i * 2, 2)
-            hi, lo = split(fv[n * 2 + dk, pair].reshape(256, 512))
+        @pl.when(y >= 0)
+        def _():
+            hi, lo = split(fv[n * 2 + dk].reshape(256, 512))
             v = dot(jnp.concatenate([hi, hi, lo], axis=1), q3[...])
-            uu[dk, n, pair] = v.reshape(2, 128, 256)
+            uu[dk, n] = v.reshape(2, 128, 256)
 
     done = []
     swaps = {}
@@ -159,43 +163,47 @@
         def __init__(self, p, half, far, near, ids, plus, minus):
             self.p, self.half, self.far, self.near = p, half, far, near
             self.ids, self.plus, self.minus = ids, plus, minus
-            self.recv = {}
-
-        def piece(self, q, h):
-            return self.p.at[q, pl.ds(h * self.half, self.half)]
-
-        def go(self, name, n, src, dst, dev):
-            cp = remote(src, dst, r_send.at[self.ids, n], r_recv.at[self.ids, n], dev)
+            self.copies = {"far0": [], "far1": [], "near": []}
+            self.count = 0
+
+        def go(self, group, q, first, size, dst, dev):
+            n = self.count
+            self.count += 1
+            cp = remote(
+                self.p.at[q, pl.ds(first, size)], dst.at[pl.ds(first, size)],
+                r_send.at[self.ids, n], r_recv.at[self.ids, n], dev,
+            )
             cp.start()
-            self.recv[name] = cp
+            self.copies[group].append(cp)
             done.append(cp)
 
-        def send_far(self):
-            self.go("f0", 0, self.piece(2, 0), self.far.at[0], self.plus)
-            self.go("f1", 1, self.piece(2, 1), self.far.at[1], self.minus)
-
-        def part(self, i, h):
-            return self.near.at[i, pl.ds(h * self.half, self.half)]
-
-        def send_plus_early(self):
-            self.go("p1", 2, self.piece(1, 1), self.part(0, 1), self.plus)
-
-        def send_minus_early(self):
-            self.go("m0", 3, self.piece(3, 0), self.part(1, 0), self.minus)
+        def send_far(self, first, size):
+            h = first // self.half
+            self.go(f"far{h}", 2, first, size, self.far, self.minus if h else self.plus)
+
+        def send_plus(self, first, size):
+            self.go("near", 1, first, size, self.near.at[0], self.plus)
+
+        def send_minus(self, first, size):
+            self.go("near", 3, first, size, self.near.at[1], self.minus)
+
+        def send_own(self):
+            for h in range(2):
+                self.send_far(h * self.half, self.half)
+            self.send_plus(self.half, self.half)
+            self.send_minus(0, self.half)
 
         def relay(self):
-            self.recv["f0"].wait_recv()
-            s = self.piece(1, 0)
-            s[...] = s[...] + self.far[0]
-            self.go("p0", 4, s, self.part(0, 0), self.plus)
-            self.recv["f1"].wait_recv()
-            s = self.piece(3, 1)
-            s[...] = s[...] + self.far[1]
-            self.go("m1", 5, s, self.part(1, 1), self.minus)
+            for h, q in ((0, 1), (1, 3)):
+                for cp in self.copies[f"far{h}"]:
+                    cp.wait_recv()
+                part = pl.ds(h * self.half, self.half)
+                self.p[q, part] = self.p[q, part] + self.far[part]
+                (self.send_minus if h else self.send_plus)(h * self.half, self.half)
 
         def finish(self):
-            for name in ("p1", "m0", "p0", "m1"):
-                self.recv[name].wait_recv()
+            for cp in self.copies["near"]:
+                cp.wait_recv()
             self.p[0] = self.p[0] + self.near[0] + self.near[1]
 
     ring_a = Ring(ua, 2, fa1, na1, 0, xp, xm)
@@ -211,22 +219,45 @@
     compute(0, 0)
     compute(1, 1)
     swap(1)
+    compute(1, 0)
     merge(0)
-    ring_a.send_far()
-    compute(1, 0)
+    ring_a.send_far(2, 1)
+    ring_b.send_far(2, 1)
+    ring_a.send_far(0, 1)
     compute(2, 1)
     swap(2)
+    compute(2, 0)
     merge(1)
-    ring_b.send_far()
-    compute(2, 0)
+    ring_b.send_far(0, 1)
+    ring_a.send_far(1, 1)
     compute(3, 1)
     swap(3)
+    compute(3, 0)
     merge(2)
-    ring_a.send_plus_early()
-    ring_a.send_minus_early()
-    ring_b.send_plus_early()
-    ring_b.send_minus_early()
-    compute(3, 0)
+    ring_a.send_far(3, 1)
+    ring_b.send_far(3, 1)
+    compute(4, 1)
+    swap(4)
+    compute(4, 0)
+    merge(3)
+    ring_b.send_far(1, 1)
+    ring_a.send_plus(2, 2)
+    ring_b.send_minus(1, 1)
+    compute(5, 1)
+    swap(5)
+    compute(5, 0)
+    merge(4)
+    ring_a.send_minus(0, 2)
+    ring_b.send_plus(2, 2)
+    compute(6, 1)
+    swap(6)
+    compute(6, 0)
+    merge(5)
+    ring_b.send_minus(0, 1)
+    compute(7, 1)
+    swap(7)
+    compute(7, 0)
+    merge(6)
     pl.semaphore_wait(plane_sem, 3)
     for i in (1, 3, 2):
         greet(all_sem, (ys[i], z, x, k))
@@ -242,19 +273,19 @@
                 cp.wait()
             store[mine] = store[mine] + dot(a[c], b[c])
 
+    ring_a.relay()
     proj(pg, gcopies, gv, pov, 0, 2)
+    merge(7)
     give_g = remote(pg.at[mine], pg.at[mine], psend.at[0], precv.at[0], partner)
     give_g.start()
-    merge(3)
-    proj(pt, hcopies, hv, piv, 0, 2)
-    ring_a.relay()
-    proj(pt, hcopies, hv, piv, 2, 4)
     ring_b.relay()
-    proj(pt, hcopies, hv, piv, 4, 7)
+    proj(pt, hcopies, hv, piv, 0, 7)
     give_t = remote(pt.at[mine], pt.at[mine], psend.at[1], precv.at[1], partner)
     give_t.start()
     done.extend((give_g, give_t))
 
+    for cp in lcopies:
+        cp.wait()
     off_row = off_ref[...].astype(f32)
     end_row = off_row + len_ref[...].astype(f32)
     off_col = jnp.transpose(jnp.broadcast_to(off_row, (8, 256)))[:, 0:1]
@@ -269,32 +300,29 @@
         lax.broadcasted_iota(jnp.int32, (PITCH, 512), 0).astype(f32) == window
     ).astype(f32)
 
+    def window_grads(first, member_here, add):
+        here = pl.ds(pl.multiple_of(first, 256), 256)
+        turned = jnp.transpose(pg[here])
+        pgt[...] = turned.reshape(8, 16, 256)
+        th, tl = split(pt[here])
+        t2 = jnp.concatenate([th, tl], axis=1)
+        for half in range(2):
+            lines = jnp.concatenate([pgt[half * 4 + k], pgt[half * 4 + 2 + k]], axis=0)
+            spread = (lines[:, None, :] * member_here[None, :, :]).reshape(32 * PITCH, 256)
+            hi, lo = split(spread)
+            grads = []
+            for i in (0, 256, 512):
+                v = dot(hi[i : i + 256], t2)
+                grads.append(v[:, 0:128] + v[:, 128:256] + dot(lo[i : i + 256], th))
+            total = jnp.concatenate(grads, axis=0).reshape(32, PITCH, 128)
+            part = pl.ds(half * 32, 32)
+            gsend[part] = gsend[part] + total if add else total
+
+    window_grads(k * 256, jnp.where(k == 0, member[:, 0:256], member[:, 256:512]), False)
     give_g.wait_recv()
     give_t.wait_recv()
-    pgt[...] = jnp.transpose(pg[...]).reshape(8, 16, 512)
-    th, tl = split(pt[...])
-    t2 = jnp.concatenate([th, tl], axis=1)
-
-    def window_grads(half):
-        lines = jnp.concatenate([pgt[half * 4 + k], pgt[half * 4 + 2 + k]], axis=0)
-        spread = (lines[:, None, :] * member[None, :, :]).reshape(32 * PITCH, 512)
-        hi, lo = split(spread)
-        grads = []
-        for i in (0, 256, 512):
-            v = dot(hi[i : i + 256], t2)
-            grads.append(v[:, 0:128] + v[:, 128:256] + dot(lo[i : i + 256], th))
-        gsend[pl.ds(half * 32, 32)] = jnp.concatenate(grads, axis=0).reshape(32, PITCH, 128)
-
-    window_grads(0)
-    ring_a.finish()
-    ring_a2.send_far()
-    ring_a2.send_plus_early()
-    ring_a2.send_minus_early()
-    ring_b.finish()
-    ring_b2.send_far()
-    ring_b2.send_plus_early()
-    ring_b2.send_minus_early()
-    window_grads(1)
+    away = ks[1]
+    window_grads(away * 256, jnp.where(k == 0, member[:, 256:512], member[:, 0:256]), True)
     pl.semaphore_wait(all_sem, 3)
 
     def spread_grads(p):
@@ -307,8 +335,14 @@
                     gssem.at[0], grsem.at[p], (ys[oy], zs[oz], xs[ox], k),
                 ).start()
 
-    for p in range(4):
-        spread_grads(p)
+    ring_a.finish()
+    ring_a2.send_own()
+    ring_b.finish()
+    ring_b2.send_own()
+    spread_grads(0)
+    spread_grads(1)
+    spread_grads(2)
+    spread_grads(3)
     grecv[48] = gsend[y * 16 + x * 4 + z]
     ring_a2.relay()
     ring_b2.relay()
@@ -377,7 +411,8 @@
     tile = jnp.sum(srecv[:, 0:4], axis=0)
     d = chip * 2 + k
     for s in range(2):
-        n = lens_ref[2 * d + s].astype(f32)
+        here = lax.broadcasted_iota(jnp.int32, (1, 256), 1) == 2 * d + s
+        n = jnp.sum(jnp.where(here, len_ref[...], 0).astype(f32), axis=1, keepdims=True)
         for j in range(2):
             line = tile[j * 2 + s : j * 2 + s + 1] * score_scale
             out_ref[s : s + 1, j * 128 : j * 128 + 128] = line / n
@@ -398,25 +433,26 @@
     return pl.pallas_call(
         kernel,
         out_shape=pltpu.VMEM((2, 256), f32),
-        in_specs=[anys] * 6 + [invm] * 2 + [pl.BlockSpec(memory_space=pltpu.SMEM)],
+        in_specs=[anys] * 8,
         out_specs=invm,
         scratch_shapes=[
-            vmem((8, 4, 128, 512), f32), vmem((512, 256), f32),
+            vmem((16, 2, 128, 512), f32), vmem((512, 256), f32),
             vmem((7, 256, KCH), bf16), vmem((7, KCH, 128), bf16),
             vmem((2, 256, KCH), bf16), vmem((2, KCH, 128), bf16),
             vmem((1536, 256), bf16),
-            vmem((2, 4, 4, 128, 256), f32), vmem((4, 4, 128, 256), f32),
+            vmem((2, 8, 2, 128, 256), f32), vmem((8, 2, 128, 256), f32),
             vmem((4, 4, 64, 256), f32), vmem((4, 4, 64, 256), f32),
-            vmem((2, 2, 64, 256), f32), vmem((2, 2, 64, 256), f32),
+            vmem((4, 64, 256), f32), vmem((4, 64, 256), f32),
             vmem((2, 4, 64, 256), f32), vmem((2, 4, 64, 256), f32),
-            vmem((2, 32, 256), f32), vmem((2, 32, 256), f32),
+            vmem((64, 256), f32), vmem((64, 256), f32),
             vmem((2, 64, 256), f32), vmem((2, 64, 256), f32),
-            vmem((512, 128), f32), vmem((512, 128), f32), vmem((8, 16, 512), f32),
+            vmem((512, 128), f32), vmem((512, 128), f32), vmem((8, 16, 256), f32),
             vmem((64, PITCH, 128), f32), vmem((64, PITCH, 128), f32),
             vmem((512, 64 * PITCH), bf16),
             vmem((64, 8, 128), f32), vmem((128, 8, 128), f32), vmem((8, 128), f32),
-            dma((8, 4)), dma((1,)), dma((2, 7)), dma((2, 2)),
-            dma((4,)), dma((4,)), dma((4, 6)), dma((4, 6)),
+            vmem((1, 256), jnp.int32), vmem((1, 256), jnp.int32),
+            dma((16, 2)), dma((1,)), dma((2,)), dma((2, 7)), dma((2, 2)),
+            dma((8,)), dma((8,)), dma((4, 10)), dma((4, 10)),
             pltpu.SemaphoreType.REGULAR, pltpu.SemaphoreType.REGULAR,
             dma((2,)), dma((2,)), dma((1,)), dma((4,)), dma((1,)), dma((1,)),
             dma((2,)),
@@ -426,7 +462,7 @@
         ),
     )(
         inverse_fisher, queries, hidden_in, proj_in, out_grad, proj_out,
-        offsets.reshape(1, 256), lengths.reshape(1, 256), lengths,
+        offsets.reshape(1, 256), lengths.reshape(1, 256),
     )
 
 

time: 43 us -> 41.6 us (0.967)
  Pallas kernels: 42.2 us -> 40.9 us
    pallas_call x1, Pallas kernels: 42.2 us -> 40.9 us  [body(): pl.pallas_call(kernel, out_shape=pltpu.VMEM((2, 256), f32), in_specs=[any...]
where the time goes in v4:
time: 41.6 us; the launch traced here: 41.5 us
  Pallas kernels  40.9 us (98%)
  local copies, waits for them, and re-layouts  0.58 us (1%)
    pallas_call x1, Pallas kernels, body(): pl.pallas_call(kernel, out_shape=pltpu.VMEM((2, 256), f32), in_specs=[any...  40.9 us

profile of v4, /device:TPU:1, one launch (start us, length us, event | category | flops | bytes accessed | tf_op | source)
XLA Modules:
  0.0 41.5 jit_solution(3979080610400268287)
XLA Ops:
  0.0 40.9 %shard_map.82 = f32[2,256]{1,0:T(2,128)S(1)} custom-call(f32[4096,512]{1,0:T(8,128)} %f_ref.1, f32[512,256]{1,0:T(8,128)} %q_ref.1, bf16[256,14336]{1,0:T(8,128)(2,1)} %h_ref.1, bf16[14336,128]{1,0:T(8,128)(2,1)} %pi_ref.1, bf16[256,4096]{1,0:T(8,128)(2,1)} %g_ref.1, bf16[4096,128]{1,0:T(8,128)(2,1)} %po_ref.1, s32[1,256]{1,0:T(1,128)} %bitcast.2, ...), custom_call_target="tpu_custom_call" | custom-call | tf_op jit(solution)/shard_map/pallas_call | solution.py:433
  40.9 0.6 %copy.10 = f32[2,256]{1,0:T(2,128)} copy(f32[2,256]{1,0:T(2,128)S(1)} %shard_map.82) | data formatting | bytes 4096

commit v5 on v4

--- a/solution.py
+++ b/solution.py
@@ -13,10 +13,6 @@
 GROUPS = (
     ((2, 2), (2, 0)), ((0, 2), (2, 1)), ((2, 3), (3, 2)), ((1, 2), (1, 3)),
     ((3, 0), (3, 1)), ((0, 3), (1, 1)), ((1, 0), (3, 3)), ((0, 1), (0, 0)),
-)
-PEERS = sorted(
-    ((i // 16, i // 4 % 4, i % 4) for i in range(1, 64)),
-    key=lambda o: -sum(min(v, 4 - v) for v in o),
 )
 PLANE = ((2, 2), (2, 1), (1, 2), (2, 3), (3, 2), (1, 1), (1, 3), (3, 1), (3, 3),
          (0, 2), (2, 0), (0, 1), (1, 0), (0, 3), (3, 0), (0, 0))
@@ -359,7 +355,10 @@
     before = jnp.sum((end_col <= col_slot).astype(f32), axis=0, keepdims=True)
     target = jnp.where(col_win < WIN, before + col_win.astype(f32), -1.0)
     line = lax.broadcasted_iota(jnp.int32, (512, 1), 0)
-    sample = (line >> 3) * 4 + ((line >> 2) & 1) * 2 + (line & 1)
+    turn = line >> 7
+    to_y = y + jnp.where(turn == 0, 2, jnp.where(turn == 1, 1, jnp.where(turn == 2, 3, 0)))
+    to_chip = (to_y & 3) * 16 + ((z + (line >> 5)) & 3) * 4 + ((x + (line >> 3)) & 3)
+    sample = to_chip * 4 + ((line >> 2) & 1) * 2 + (line & 1)
     oneh[...] = (sample.astype(f32) == target).astype(f32).astype(bf16)
 
     def gather_grads(first, count):
@@ -370,32 +369,40 @@
         part = pl.ds(first * PITCH, count * PITCH)
         gh, gl = split(grecv[first : first + count].reshape(count * PITCH, 128))
         gg = jnp.concatenate([gh, gl], axis=1)
-        both = [dot(oneh[i : i + 256, part], gg) for i in (0, 256)]
-        return [v[:, 0:128] + v[:, 128:256] for v in both]
+
+        def product(i):
+            v = dot(oneh[i * 256 : i * 256 + 256, part], gg)
+            return v[:, 0:128] + v[:, 128:256]
+
+        return product
 
     ring_a2.finish()
     ring_b2.finish()
-    dense_a = gather_grads(0, 32)
+    product_a = gather_grads(0, 32)
+    dense_a = [product_a(i) for i in range(2)]
 
     uh, ul = split(jnp.concatenate([ua[0, 0], ub[0, 0]], axis=0))
     u3 = jnp.concatenate([uh, ul, uh], axis=0)
 
-    dense_b = gather_grads(32, 32)
+    product_b = gather_grads(32, 32)
     upper = ((line[0:256] >> 1) & 1) == 0
     for i in range(2):
-        dh, dl = split(dense_a[i] + dense_b[i])
+        dh, dl = split(dense_a[i] + product_b(i))
         both = dot(jnp.concatenate([dh, dh, dl], axis=1), u3)
         tiles = jnp.where(upper, both[:, 0:128], both[:, 128:256])
         sbuf[i * 32 : i * 32 + 32] = tiles.reshape(32, 8, 128)
-
-    for oy, oz, ox in PEERS:
-        for kk in range(2):
-            remote(
-                sbuf.at[ys[oy] * 16 + zs[oz] * 4 + xs[ox], pl.ds(kk * 4, 4)],
-                srecv.at[k * 64 + chip, pl.ds(0, 4)],
-                sssem.at[0], srsem.at[0], (ys[oy], zs[oz], xs[ox], kk),
-            ).start()
-    own = sbuf[chip]
+        for p in (2 * i, 2 * i + 1):
+            oy = TURNS[p]
+            for oz, ox in PLANE:
+                for kk in range(2):
+                    if (oy, oz, ox) != (0, 0, 0):
+                        remote(
+                            sbuf.at[p * 16 + oz * 4 + ox, pl.ds(kk * 4, 4)],
+                            srecv.at[k * 64 + chip, pl.ds(0, 4)],
+                            sssem.at[0], srsem.at[0], (ys[oy], zs[oz], xs[ox], kk),
+                        ).start()
+
+    own = sbuf[48]
     srecv[k * 64 + chip, 0:4] = jnp.where(k == 0, own[0:4], own[4:8])
     other[0:4] = jnp.where(k == 0, own[4:8], own[0:4])
     last = remote(

time: 41.6 us -> 41.7 us (level)
  no operation moved by 1% of the time
where the time goes in v5:
time: 41.7 us; the launch traced here: 41.6 us
  Pallas kernels  41 us (98%)
  local copies, waits for them, and re-layouts  0.58 us (1%)
    pallas_call x1, Pallas kernels, body(): pl.pallas_call(kernel, out_shape=pltpu.VMEM((2, 256), f32), in_specs=[any...  41 us

profile of v5, /device:TPU:1, one launch (start us, length us, event | category | flops | bytes accessed | tf_op | source)
XLA Modules:
  0.0 41.6 jit_solution(9447257354584295474)
XLA Ops:
  0.0 41.0 %shard_map.82 = f32[2,256]{1,0:T(2,128)S(1)} custom-call(f32[4096,512]{1,0:T(8,128)} %f_ref.1, f32[512,256]{1,0:T(8,128)} %q_ref.1, bf16[256,14336]{1,0:T(8,128)(2,1)} %h_ref.1, bf16[14336,128]{1,0:T(8,128)(2,1)} %pi_ref.1, bf16[256,4096]{1,0:T(8,128)(2,1)} %g_ref.1, bf16[4096,128]{1,0:T(8,128)(2,1)} %po_ref.1, s32[1,256]{1,0:T(1,128)} %bitcast.2, ...), custom_call_target="tpu_custom_call" | custom-call | tf_op jit(solution)/shard_map/pallas_call | solution.py:440
  41.0 0.6 %copy.10 = f32[2,256]{1,0:T(2,128)} copy(f32[2,256]{1,0:T(2,128)S(1)} %shard_map.82) | data formatting | bytes 4096
